TPU v7x, 512 devices: a whole 4x8x8 slice. The times are simulated.
512 devices in a mesh: dp: 64 (over z, y_hi, core), stat: 8 (over x, y_lo).
Axes of the slice: x: 4, y: 8 (y_hi: 4, y_lo: 2; y = y_hi * 2 + y_lo), z: 8, core: 2. Of those that a mesh axis runs over, the one named last changes fastest.
Arguments:
- activations: bfloat16 [65536, 8192], P('dp'), may hold values from -16 to 16
- out_grads: bfloat16 [65536, 1024], P('dp', 'stat'), may hold values from -0.0234375 to 0.0234375
- stat_old: float32 [192, 128, 128], P('dp'), may hold values from -0.24 to 0.24
- pattern: int32 [192, 2], replicated, may hold values from 0 to 63, as said below
- holders: int32 [192], replicated, may hold values from 0 to 63, as said below
Outputs:
- direction: float32 [8192, 1024], P('dp', 'stat')
- statistics: float32 [192, 128, 128], P('dp', 'stat')
Inputs may be any that keep to these rules, and one draw needn't show every extreme that they name: `pattern`: every diagonal pair (a, a) for a in 0 to 63 appears exactly once; every other entry has different row and column blocks; half of those are band pairs (column block next to the row block, cyclically), the rest reach anywhere. `holders`: every dp index holds exactly 3 entries; the diagonal entry (a, a) is held by the dp index whose weight rows contain row a * 128.
All inputs are finite; a program needn't handle non-finite values.
Results may differ from a plain program's by a relative error of at most 0.003.
Values may be sent and summed in bfloat16 or wider, within the bound.
No kernel may reach another device: no remote copies, remote signals or barrier semaphores. Data moves between devices by JAX's collectives and lax.ppermute only.
A program may use at most 192 MiB of HBM per device.

v0:
```python
import jax
import jax.numpy as jnp
from jax import lax
from jax.sharding import PartitionSpec as P

ITERS = 5


beta_stat = 0.6
damping = 0.75


def inverse_root(matrix):
    size = matrix.shape[0]
    eye = jnp.eye(size, dtype=matrix.dtype)
    sym = 0.5 * (matrix + matrix.T) + damping * eye
    scale = jnp.sqrt(jnp.sum(sym * sym))
    current = sym / scale
    result = eye
    for sweep in range(ITERS):
        factor = (5.0 * eye - current) * 0.25
        result = jnp.dot(result, factor, precision=lax.Precision.HIGHEST)
        square = jnp.dot(factor, factor, precision=lax.Precision.HIGHEST)
        fourth = jnp.dot(square, square, precision=lax.Precision.HIGHEST)
        current = jnp.dot(fourth, current, precision=lax.Precision.HIGHEST)
    return result * scale ** (-0.25)


def per_device(activations, out_grads, stat_old, pattern, holders):
    position = lax.axis_index("dp")
    stat_pos = lax.axis_index("stat")
    stat_count = lax.axis_size("stat")
    group_count = lax.axis_size("dp")
    block = stat_old.shape[2]
    held = stat_old.shape[0]
    width_cols = out_grads.shape[1]
    total_cols = width_cols * stat_count
    own_rows = activations.shape[1] // group_count
    own_panels = own_rows // block
    share_rows = block // stat_count
    partial_value = lax.dot_general(
        activations, out_grads, (((0,), (0,)), ((), ())), preferred_element_type=jnp.float32
    )
    grad_own = lax.psum_scatter(partial_value, "dp", scatter_dimension=0, tiled=True)
    grad_b = grad_own.astype(jnp.bfloat16)
    grad_full = lax.all_gather(grad_b, "dp", axis=0, tiled=True)
    entries = jnp.arange(holders.shape[0], dtype=jnp.int32)
    same_holder = holders[None, :] == holders[:, None]
    earlier = entries[None, :] < entries[:, None]
    within = jnp.sum((same_holder & earlier).astype(jnp.int32), axis=1)
    slot_ids = jnp.arange(held, dtype=jnp.int32)
    picked = ((holders[None, :] == position) & (within[None, :] == slot_ids[:, None])).astype(
        jnp.int32
    )
    row_blocks = jnp.sum(picked * pattern[None, :, 0], axis=1)
    col_blocks = jnp.sum(picked * pattern[None, :, 1], axis=1)

    def panel_at(index):
        return lax.dynamic_slice_in_dim(grad_full, index * block, block, 0)

    first = jax.vmap(panel_at)(row_blocks)
    second = jax.vmap(panel_at)(col_blocks)
    partial_gram = jnp.einsum("jrc,jsc->jrs", first, second, preferred_element_type=jnp.float32)
    panel_ids = position * own_panels + jnp.arange(own_panels, dtype=jnp.int32)
    select = (
        (row_blocks[None, :] == panel_ids[:, None]) & (col_blocks[None, :] == panel_ids[:, None])
    ).astype(jnp.float32)
    gram = lax.psum(partial_gram, "stat") / total_cols
    new_full = beta_stat * stat_old + (1.0 - beta_stat) * gram
    statistics = lax.dynamic_slice_in_dim(new_full, stat_pos * share_rows, share_rows, 1)
    diag_full = jnp.einsum("ij,jrs->irs", select, new_full, precision=lax.Precision.HIGHEST)
    roots = jax.vmap(inverse_root)(diag_full)
    stacked = grad_b.reshape(own_panels, block, width_cols).astype(jnp.float32)
    direction = jnp.einsum("irs,isc->irc", roots, stacked, precision=lax.Precision.HIGHEST).reshape(
        own_rows, width_cols
    )
    return (direction, statistics)


def solution(mesh):
    placed = (P("dp", None), P("dp", "stat"), P("dp", None, None), P(), P())
    return jax.shard_map(
        per_device,
        mesh=mesh,
        in_specs=placed,
        out_specs=(P("dp", "stat"), P("dp", "stat", None)),
        check_vma=False,
    )
```

profile of v0, /device:TPU:1, one launch (start us, length us, event | category | flops | bytes accessed | tf_op | source)
XLA Modules:
  0.0 367.6 jit_solution(4225835935777401481)
XLA Ops:
  7.2 0.9 copy-done
  8.1 10.1 %fusion.82 = f32[8192,128]{1,0:T(8,128)} fusion(bf16[1024,8192]{1,0:T(8,128)(2,1)} %param.5, bf16[1024,128]{1,0:T(8,128)(2,1)S(1)} %copy-done), kind=kOutput, calls=%fused_computation.101 | convolution fusion | flops 2147483648 | bytes 21233664 | tf_op jit(solution)/shard_map/dot_general | solution.py:41
  18.3 157.9 %reduce-scatter.2.cloned.1.call-done = f32[128,128]{1,0:T(8,128)} async-done(((f32[8192,128]{1,0:T(8,128)}), f32[128,128]{1,0:T(8,128)}) %reduce-scatter.2.cloned.1.call-update) | async-done | bytes 65552 | tf_op jit(solution)/shard_map/reduce_scatter | solution.py:44
  176.2 1.5 convert_element_type.5
  178.1 88.0 %all-gather.2.cloned.1.call-done = bf16[8192,128]{1,0:T(8,128)(2,1)} async-done(((bf16[128,128]{1,0:T(8,128)(2,1)}), bf16[8192,128]{1,0:T(8,128)(2,1)}) %all-gather.2.cloned.1.call-update) | async-done | bytes 2097168 | tf_op jit(solution)/shard_map/all_gather | solution.py:46
  266.1 5.7 %while.2 = (s32[]{:T(128)}, bf16[8192,128]{1,0:T(8,128)(2,1)}, s32[3,2]{0,1:T(2,128)S(1)}, bf16[3,128,128]{2,1,0:T(8,128)(2,1)S(1)}, s32[]{:T(128)}) while((s32[]{:T(128)}, bf16[8192,128]{1,0:T(8,128)(2,1)}, s32[3,2]{0,1:T(2,128)S(1)}, bf16[3,128,128]{2,1,0:T(8,128)(2,1)S(1)}, s32[]{:T(128)}) %tuple.34), condition=%wide.while_cond, body=%wide.while_body.sunk | while | flops 2 | bytes 65641 | solution.py:59
  266.2 0.5 slice.34
  266.7 1.3 bitcast_dynamic-update-slice_fusion.4
  268.1 0.5 slice.34
  268.6 1.3 bitcast_dynamic-update-slice_fusion.4
  270.5 1.3 bitcast_dynamic-update-slice_fusion.4
  271.9 6.1 %while.3 = (s32[]{:T(128)}, bf16[8192,128]{1,0:T(8,128)(2,1)}, s32[3,2]{0,1:T(2,128)S(1)}, bf16[3,128,128]{2,1,0:T(8,128)(2,1)S(1)}, s32[]{:T(128)}) while((s32[]{:T(128)}, bf16[8192,128]{1,0:T(8,128)(2,1)}, s32[3,2]{0,1:T(2,128)S(1)}, bf16[3,128,128]{2,1,0:T(8,128)(2,1)S(1)}, s32[]{:T(128)}) %tuple.46), condition=%wide.while_cond.1, body=%wide.while_body.1.sunk | while | flops 2 | bytes 65641 | solution.py:59
  272.0 0.5 slice.35
  272.5 1.4 bitcast_dynamic-update-slice_fusion.5
  274.0 0.5 slice.35
  274.5 1.4 bitcast_dynamic-update-slice_fusion.5
  276.1 0.5 slice.35
  276.6 1.4 bitcast_dynamic-update-slice_fusion.5
  278.0 0.9 fusion.83
  278.9 74.2 %all-reduce.4.cloned.1.call-done = f32[3,128,128]{2,1,0:T(8,128)} async-done(((f32[3,128,128]{2,1,0:T(8,128)}), f32[3,128,128]{2,1,0:T(8,128)}) %all-reduce.4.cloned.1.call-update) | async-done | bytes 196624 | tf_op jit(solution)/shard_map/psum | solution.py:68
  353.1 1.0 multiply_add_fusion
  354.6 0.6 multiply_reduce_fusion
  359.6 0.8 fusion.90
  360.4 0.6 constant_dynamic-slice_fusion.2
  (51 shorter events, 5.6 us)
Async XLA Ops:
  7.2 1.0 copy-start
  7.2 169.0 %reduce-scatter.2.cloned.1.call-start = ((), (), s32[]{:S(2)}) async-start(), calls=%async_computation.1 | async-start | bytes 4259840 | tf_op jit(solution)/shard_map/reduce_scatter | solution.py:44
  18.2 159.5 %copy-start.3 = (s32[192]{0:T(256)S(1)}, s32[192]{0:T(256)}, u32[]{:S(2)}) copy-start(s32[192]{0:T(256)} %param.9) | copy-start | bytes 2308
  18.2 159.7 %copy-start.4 = (s32[192,2]{0,1:T(2,128)S(1)}, s32[192,2]{0,1:T(2,128)}, u32[]{:S(2)}) copy-start(s32[192,2]{0,1:T(2,128)} %param.8) | copy-start | bytes 4612
  18.2 334.9 %copy-start.2 = (f32[3,128,128]{2,1,0:T(8,128)S(1)}, f32[3,128,128]{2,1,0:T(8,128)}, u32[]{:S(2)}) copy-start(f32[3,128,128]{2,1,0:T(8,128)} %param.7) | copy-start | bytes 589828
  18.2 247.9 %all-gather.2.cloned.1.call-start = ((), (), s32[]{:S(2)}) async-start(), calls=%async_computation.2 | async-start | bytes 2129920 | tf_op jit(solution)/shard_map/all_gather | solution.py:46
  177.6 182.0 %copy-start.1 = (bf16[128,128]{1,0:T(8,128)(2,1)S(1)}, bf16[128,128]{1,0:T(8,128)(2,1)}, u32[]{:S(2)}) copy-start(bf16[128,128]{1,0:T(8,128)(2,1)} %convert_element_type.5) | copy-start | bytes 98308
  177.7 175.4 %all-reduce.4.cloned.1.call-start = ((), (), s32[]{:S(2)}) async-start(), calls=%async_computation.3 | async-start | bytes 393216 | tf_op jit(solution)/shard_map/psum | solution.py:68
Sparse Core Ops, SparseCore 0:
  18.4 157.7 reduce-scatter.1
  180.1 85.9 all-gather.1
  279.0 74.0 all-reduce.3
where the time goes:
time: 373 us; the launch traced here: 368 us
  waiting for transfers between devices  320 us (86%)
  matrix products  15.7 us (4%)
  between operations  14.8 us (4%)
  local copies, waits for them, and re-layouts  13.4 us (4%)
    reduce_scatter x1, waiting for transfers between devices, per_device(): lax.psum_scatter(partial_value, 'dp', scatter_dimension=0, tiled=True)  158 us
    all_gather x1, waiting for transfers between devices, per_device(): grad_full = lax.all_gather(grad_b, 'dp', axis=0, tiled=True)  88 us
    psum x1, waiting for transfers between devices, per_device(): gram = lax.psum(partial_gram, 'stat') / total_cols  74.2 us
    gather x18, local copies, waits for them, and re-layouts  11.7 us
    dot_general x1, matrix products, per_device(): lax.dot_general(activations, out_grads, (((0,), (0,)), ((), ())), preferr...  10.1 us
  transfers between devices with their start and end apart: 3, of which 3 were waited for; matrix products, arithmetic and copies ran while one was open for 0% of the time, Pallas kernels for 0%

commit v1 on v0

v1 whole, which is shorter than its diff:
```python
import jax
import jax.numpy as jnp
from jax import lax
from jax.sharding import PartitionSpec as P

ITERS = 5
beta_stat = 0.6
damping = 0.75

NZ, NY, NC = 8, 4, 2
Z_GROUPS = [[z * NY * NC + r for z in range(NZ)] for r in range(NY * NC)]
Y_GROUPS = [[(z * NY + y) * NC + c for y in range(NY)] for z in range(NZ) for c in range(NC)]

f32 = jnp.float32
bf16 = jnp.bfloat16
HI = lax.Precision.HIGHEST


def inverse_root(matrix):
    size = matrix.shape[0]
    eye = jnp.eye(size, dtype=matrix.dtype)
    sym = 0.5 * (matrix + matrix.T) + damping * eye
    scale = jnp.sqrt(jnp.sum(sym * sym))
    current = sym / scale
    result = eye
    for sweep in range(ITERS):
        factor = (5.0 * eye - current) * 0.25
        if sweep == 0:
            result = factor
        else:
            result = jnp.dot(result, factor, precision=HI)
        if sweep < ITERS - 1:
            square = jnp.dot(factor, factor, precision=HI)
            fourth = jnp.dot(square, square, precision=HI)
            current = jnp.dot(fourth, current, precision=HI)
    return result * scale ** (-0.25)


def exchange(x, axis, groups=None):
    return lax.all_to_all(x, axis, 0, 0, axis_index_groups=groups, tiled=True)


def tables(pattern, holders, position, held, n_dp):
    rows, cols = pattern[:, 0], pattern[:, 1]
    entries = jnp.arange(holders.shape[0], dtype=jnp.int32)
    off = rows != cols
    same = (holders[None, :] == holders[:, None]) & (entries[None, :] < entries[:, None])
    within = jnp.sum(same.astype(jnp.int32), axis=1)
    rank = jnp.sum((same & off[None, :]).astype(jnp.int32), axis=1)
    dests = jnp.arange(n_dp, dtype=jnp.int32)
    mine = off[None, :] & (holders[None, :] == dests[:, None])
    needs = [dests, dests]
    for m in range(held - 1):
        hit = (mine & (rank[None, :] == m)).astype(jnp.int32)
        needs.append(jnp.sum(hit * rows[None, :], axis=1))
        needs.append(jnp.sum(hit * cols[None, :], axis=1))
    diag_slot = jnp.sum(jnp.where((~off) & (holders == position), within, 0))
    return needs, diag_slot


def per_device(activations, out_grads, stat_old, pattern, holders):
    position = lax.axis_index("dp")
    stat_pos = lax.axis_index("stat")
    n_stat = lax.axis_size("stat")
    n_dp = NZ * NY * NC
    block = stat_old.shape[2]
    held = stat_old.shape[0]
    width = out_grads.shape[1]
    rows = activations.shape[1]
    panels = rows // block
    half = panels // NC
    zr = block // NZ
    yr = zr // NY
    share = block // n_stat
    core = position % NC

    partial = lax.dot_general(
        activations, out_grads, (((0,), (0,)), ((), ())), preferred_element_type=f32
    ).reshape(NC, half * block, width)
    give = lax.dynamic_index_in_dim(partial, 1 - core, 0, keepdims=False)
    keep = lax.dynamic_index_in_dim(partial, core, 0, keepdims=False)
    got = lax.ppermute(give, "dp", [(i, i ^ 1) for i in range(n_dp)])
    pair = (keep + got).reshape(half, NZ, zr, width).transpose(1, 0, 2, 3)
    pair = exchange(pair.astype(bf16).reshape(NZ, half * zr, width), "dp", Z_GROUPS)
    line = jnp.sum(pair.astype(f32), axis=0).reshape(half, NY, yr, width)
    line = line.transpose(1, 0, 2, 3).reshape(NY, half * yr, width)
    owned = jnp.sum(exchange(line, "dp", Y_GROUPS), axis=0)
    owned = owned.reshape(half, yr * width)

    needs, diag_slot = tables(pattern, holders, position, held, n_dp)
    high = owned.astype(bf16)
    low = (owned - high.astype(f32)).astype(bf16)
    local = jnp.arange(half, dtype=jnp.int32) + core * half
    sent = []
    for k, need in enumerate(needs):
        pick = (need[:, None] == local[None, :]).astype(bf16)
        sent.append(jnp.dot(pick, low if k == 1 else high, preferred_element_type=f32).astype(bf16))
    kinds = len(sent)
    sent = jnp.stack(sent, axis=1).reshape(n_dp, kinds * yr, width)
    came = exchange(sent, "dp").reshape(NZ * NY, NC, kinds, yr, width)
    came = (came[:, 0] + came[:, 1]).transpose(1, 0, 2, 3).reshape(kinds, block, width)

    def gram_of(a, b):
        return lax.dot_general(a, b, (((1,), (1,)), ((), ())), preferred_element_type=f32)

    diag = jnp.broadcast_to(gram_of(came[0], came[0])[None], (n_stat, block, block))
    others = [
        gram_of(came[2 + 2 * m], came[3 + 2 * m]).reshape(n_stat, share, block)
        for m in range(held - 1)
    ]
    grams = exchange(jnp.concatenate([diag] + others, axis=1), "stat")
    grams = jnp.sum(grams, axis=0) * ((1.0 - beta_stat) / (width * n_stat))

    old_diag = lax.dynamic_index_in_dim(stat_old, diag_slot, 0, keepdims=False)
    new_diag = beta_stat * old_diag + grams[:block]
    root = inverse_root(new_diag)
    grad = came[0].astype(f32) + came[1].astype(f32)
    direction = jnp.dot(root, grad, precision=HI)

    diag_rows = lax.dynamic_slice_in_dim(grams[:block], stat_pos * share, share, 0)
    slots = []
    for j in range(held):
        part = diag_rows
        for m in range(held - 1):
            here = (diag_slot != j) & (jnp.where(diag_slot < j, j - 1, j) == m)
            part = jnp.where(here, grams[block + m * share : block + (m + 1) * share], part)
        slots.append(part)
    old_rows = lax.dynamic_slice_in_dim(stat_old, stat_pos * share, share, 1)
    statistics = beta_stat * old_rows + jnp.stack(slots)
    return (direction, statistics)


def solution(mesh):
    placed = (P("dp", None), P("dp", "stat"), P("dp", None, None), P(), P())
    return jax.shard_map(
        per_device,
        mesh=mesh,
        in_specs=placed,
        out_specs=(P("dp", "stat"), P("dp", "stat", None)),
        check_vma=False,
    )
```

time: 373 us -> 130 us (0.35); the launches traced: 368 us -> 129 us
  waiting for transfers between devices: 320 us -> 45 us
  blocking collectives: 0 us -> 24.3 us
  starting transfers between devices: 0.12 us -> 24.3 us
  between operations: 14.8 us -> 6.98 us
  local copies, waits for them, and re-layouts: 13.4 us -> 8.18 us
    reduce_scatter x1 -> x0, waiting for transfers between devices: 158 us -> none  [per_device(): lax.psum_scatter(partial_value, 'dp', scatter_dimension=0, tiled=True)]
    all_gather x1 -> x0, waiting for transfers between devices: 88 us -> none  [per_device(): grad_full = lax.all_gather(grad_b, 'dp', axis=0, tiled=True)]
    psum x1 -> x0, waiting for transfers between devices: 74.2 us -> none  [per_device(): gram = lax.psum(partial_gram, 'stat') / total_cols]
    all_to_all x0 -> x3, waiting for transfers between devices: none -> 41.1 us  [exchange(): return lax.all_to_all(x, axis, 0, 0, axis_index_groups=groups, tiled=True)]
    all_to_all x0 -> x1, blocking collectives: none -> 24.3 us  [exchange(): return lax.all_to_all(x, axis, 0, 0, axis_index_groups=groups, tiled=True)]
    all_to_all x0 -> x3, starting transfers between devices: none -> 15.5 us  [exchange(): return lax.all_to_all(x, axis, 0, 0, axis_index_groups=groups, tiled=True)]
    gather x18 -> x0, local copies, waits for them, and re-layouts: 11.7 us -> none
    ppermute x0 -> x1, starting transfers between devices: none -> 8.73 us  [per_device(): got = lax.ppermute(give, 'dp', [(i, i ^ 1) for i in range(n_dp)])]
  transfers between devices with their start and end apart: 3 -> 4, of which waited for: 3 -> 4; matrix products, arithmetic and copies ran while one was open for 0% -> 2% of each run, Pallas kernels for 0% -> 0%
where the time goes in v1:
time: 130 us; the launch traced here: 129 us
  waiting for transfers between devices  45 us (35%)
  starting transfers between devices  24.3 us (19%)
  blocking collectives  24.3 us (19%)
  matrix products  13.9 us (11%)
  local copies, waits for them, and re-layouts  8.18 us (6%)
  between operations  6.98 us (5%)
  other arithmetic  6.15 us (5%)
    all_to_all x3, waiting for transfers between devices, exchange(): return lax.all_to_all(x, axis, 0, 0, axis_index_groups=groups, tiled=True)  41.1 us
    all_to_all x1, blocking collectives, exchange(): return lax.all_to_all(x, axis, 0, 0, axis_index_groups=groups, tiled=True)  24.3 us
    all_to_all x3, starting transfers between devices, exchange(): return lax.all_to_all(x, axis, 0, 0, axis_index_groups=groups, tiled=True)  15.5 us
    ppermute x1, starting transfers between devices, per_device(): got = lax.ppermute(give, 'dp', [(i, i ^ 1) for i in range(n_dp)])  8.73 us
    dot_general x1, matrix products, per_device(): lax.dot_general(activations, out_grads, (((0,), (0,)), ((), ())), preferr...  8.24 us
    ppermute x1, waiting for transfers between devices, per_device(): got = lax.ppermute(give, 'dp', [(i, i ^ 1) for i in range(n_dp)])  3.94 us
    unnamed x9, local copies, waits for them, and re-layouts  2.95 us
  transfers between devices with their start and end apart: 4, of which 4 were waited for; matrix products, arithmetic and copies ran while one was open for 2% of the time, Pallas kernels for 0%

profile of v1, /device:TPU:1, one launch (start us, length us, event | category | flops | bytes accessed | tf_op | source)
XLA Modules:
  0.0 128.9 jit_solution(1193355499063863009)
XLA Ops:
  0.7 0.9 copy-done
  1.6 8.2 %fusion.102 = f32[8192,128]{1,0:T(8,128)S(1)} fusion(bf16[1024,8192]{1,0:T(8,128)(2,1)} %param.5, bf16[1024,128]{1,0:T(8,128)(2,1)S(1)} %copy-done), kind=kOutput, calls=%fused_computation.137 | convolution fusion | flops 2147483648 | bytes 21233664 | tf_op jit(solution)/shard_map/dot_general | solution.py:77
  9.8 1.9 %copy-done.1 = f32[8192,128]{1,0:T(8,128)} copy-done((f32[8192,128]{1,0:T(8,128)}, f32[8192,128]{1,0:T(8,128)S(1)}, u32[]{:S(2)}) %copy-start.1) | copy-done | bytes 4194328
  11.8 1.5 %dynamic-slice_bitcast_fusion = f32[4096,128]{1,0:T(8,128)} fusion(f32[2,4096,128]{2,1,0:T(8,128)S(1)} %bitcast.109, s32[]{:T(128)S(6)} %select_n.81), kind=kLoop, calls=%fused_computation.3 | loop fusion | bytes 4194308 | tf_op jit(solution)/shard_map/jit(dynamic_index_in_dim)/squeeze | solution.py:80
  13.2 8.7 %collective-permute-start = (f32[4096,128]{1,0:T(8,128)}, f32[4096,128]{1,0:T(8,128)S(1)}, u32[]{:S(2)}, u32[]{:S(2)}) collective-permute-start(f32[4096,128]{1,0:T(8,128)} %dynamic-slice_bitcast_fusion), channel_id=1, source_target_pairs={{0,8},{8,0},{16,24},{24,16},{32,40},{40,32},{48,56},{56,48},{64,72... | collective-permute-start | bytes 6291464 | tf_op jit(solution)/shard_map/ppermute | solution.py:82
  22.0 3.9 %collective-permute-done = f32[4096,128]{1,0:T(8,128)S(1)} collective-permute-done((f32[4096,128]{1,0:T(8,128)}, f32[4096,128]{1,0:T(8,128)S(1)}, u32[]{:S(2)}, u32[]{:S(2)}) %collective-permute-start) | collective-permute-done | bytes 2097184 | tf_op jit(solution)/shard_map/ppermute | solution.py:82
  25.9 1.8 %fusion = bf16[4096,128]{1,0:T(8,128)(2,1)S(1)} fusion(f32[4096,128]{1,0:T(8,128)S(1)} %collective-permute-done, f32[2,4096,128]{2,1,0:T(8,128)} %bitcast.110, s32[]{:T(128)S(6)} %select_n.80), kind=kLoop, calls=%fused_computation.1 | loop fusion | flops 1048576 | bytes 5242884 | tf_op jit(solution)/shard_map/convert_element_type | solution.py:84
  27.7 1.2 copy.32
  28.9 4.7 %all-to-all-start = ((bf16[8,512,128]{2,1,0:T(8,128)(2,1)}), bf16[8,512,128]{2,1,0:T(8,128)(2,1)S(1)}, u32[]{:S(2)}, u32[]{:S(2)}) async-start(bf16[8,512,128]{2,1,0:T(8,128)(2,1)} %bitcast.8), calls=%async_computation | async-start | bytes 2097152 | tf_op jit(solution)/shard_map/all_to_all | solution.py:40
  33.9 29.0 %all-to-all-done = bf16[8,512,128]{2,1,0:T(8,128)(2,1)S(1)} async-done(((bf16[8,512,128]{2,1,0:T(8,128)(2,1)}), bf16[8,512,128]{2,1,0:T(8,128)(2,1)S(1)}, u32[]{:S(2)}, u32[]{:S(2)}) %all-to-all-start) | async-done | bytes 1048608 | tf_op jit(solution)/shard_map/all_to_all | solution.py:40
  63.0 0.7 copy.33
  63.7 6.8 %all-to-all-start.1 = ((f32[4,128,128]{2,1,0:T(8,128)}), f32[4,128,128]{2,1,0:T(8,128)S(1)}, u32[]{:S(2)}, u32[]{:S(2)}) async-start(f32[4,128,128]{2,1,0:T(8,128)} %bitcast.11), calls=%async_computation.1 | async-start | bytes 524288 | tf_op jit(solution)/shard_map/all_to_all | solution.py:40
  70.7 8.3 %all-to-all-done.1 = f32[4,128,128]{2,1,0:T(8,128)S(1)} async-done(((f32[4,128,128]{2,1,0:T(8,128)}), f32[4,128,128]{2,1,0:T(8,128)S(1)}, u32[]{:S(2)}, u32[]{:S(2)}) %all-to-all-start.1) | async-done | bytes 262176 | tf_op jit(solution)/shard_map/all_to_all | solution.py:40
  80.2 0.2 copy.34
  80.4 0.2 reshape.86
  80.7 24.3 %all_to_all.20 = bf16[64,24,128]{2,1,0:T(8,128)(2,1)S(1)} all-to-all(bf16[64,24,128]{2,1,0:T(8,128)(2,1)S(1)} %reshape.86), channel_id=1, replica_groups=mesh['dp'=64,'stat'=8] {'dp'}, dimensions={0} | all-to-all | bytes 786432 | tf_op jit(solution)/shard_map/all_to_all | solution.py:40
  105.7 0.9 pad_maximum_fusion
  106.5 4.0 %all-to-all-start.3 = ((f32[8,160,128]{2,1,0:T(8,128)}), f32[8,160,128]{2,1,0:T(8,128)S(1)}, u32[]{:S(2)}, u32[]{:S(2)}) async-start(f32[8,160,128]{2,1,0:T(8,128)} %pad_maximum_fusion), calls=%async_computation.3 | async-start | bytes 1310720 | tf_op jit(solution)/shard_map/all_to_all | solution.py:40
  110.5 0.6 fusion.77
  116.4 0.8 constant_dynamic-slice_fusion
  117.4 3.9 %all-to-all-done.3 = f32[8,160,128]{2,1,0:T(8,128)S(1)} async-done(((f32[8,160,128]{2,1,0:T(8,128)}), f32[8,160,128]{2,1,0:T(8,128)S(1)}, u32[]{:S(2)}, u32[]{:S(2)}) %all-to-all-start.3) | async-done | bytes 655392 | tf_op jit(solution)/shard_map/all_to_all | solution.py:40
  121.5 0.6 multiply_reduce_fusion
  126.7 0.8 fusion.20
  127.5 1.4 %maximum_add_fusion = f32[3,16,128]{2,1,0:T(8,128)} fusion(f32[1,16,128]{2,1,0:T(8,128)S(1)} %copy.39, f32[1,16,128]{2,1,0:T(8,128)S(1)} %copy.38, f32[1,16,128]{2,1,0:T(8,128)S(1)} %copy.37, f32[3,128,128]{2,1,0:T(8,128)} %param.7, s32[]{:T(128)S(6)} %select_n.82), kind=kLoop, calls=%fused_computation.96 | loop fusion | flops 24576 | bytes 73732 | tf_op jit(solution)/shard_map/add | solution.py:129
  (55 shorter events, 6.4 us)
Async XLA Ops:
  0.6 1.0 copy-start
  9.8 1.9 %copy-start.1 = (f32[8192,128]{1,0:T(8,128)}, f32[8192,128]{1,0:T(8,128)S(1)}, u32[]{:S(2)}) copy-start(f32[8192,128]{1,0:T(8,128)S(1)} %fusion.102) | copy-start | bytes 12582916
  13.2 12.7 %collective-permute-start = (f32[4096,128]{1,0:T(8,128)}, f32[4096,128]{1,0:T(8,128)S(1)}, u32[]{:S(2)}, u32[]{:S(2)}) collective-permute-start(f32[4096,128]{1,0:T(8,128)} %dynamic-slice_bitcast_fusion), channel_id=1, source_target_pairs={{0,8},{8,0},{16,24},{24,16},{32,40},{40,32},{48,56},{56,48},{64,72... | collective-permute-start | bytes 6291464 | tf_op jit(solution)/shard_map/ppermute | solution.py:82
  22.0 11.6 %copy-start.3 = (s32[192,2]{0,1:T(2,128)S(1)}, s32[192,2]{0,1:T(2,128)}, u32[]{:S(2)}) copy-start(s32[192,2]{0,1:T(2,128)} %param.8) | copy-start | bytes 4612
  22.0 11.7 %copy-start.2 = (s32[192]{0:T(256)S(1)}, s32[192]{0:T(256)}, u32[]{:S(2)}) copy-start(s32[192]{0:T(256)} %param.9) | copy-start | bytes 2308
  28.9 33.9 %all-to-all-start = ((bf16[8,512,128]{2,1,0:T(8,128)(2,1)}), bf16[8,512,128]{2,1,0:T(8,128)(2,1)S(1)}, u32[]{:S(2)}, u32[]{:S(2)}) async-start(bf16[8,512,128]{2,1,0:T(8,128)(2,1)} %bitcast.8), calls=%async_computation | async-start | bytes 2097152 | tf_op jit(solution)/shard_map/all_to_all | solution.py:40
  63.7 15.2 %all-to-all-start.1 = ((f32[4,128,128]{2,1,0:T(8,128)}), f32[4,128,128]{2,1,0:T(8,128)S(1)}, u32[]{:S(2)}, u32[]{:S(2)}) async-start(f32[4,128,128]{2,1,0:T(8,128)} %bitcast.11), calls=%async_computation.1 | async-start | bytes 524288 | tf_op jit(solution)/shard_map/all_to_all | solution.py:40
  106.5 14.7 %all-to-all-start.3 = ((f32[8,160,128]{2,1,0:T(8,128)}), f32[8,160,128]{2,1,0:T(8,128)S(1)}, u32[]{:S(2)}, u32[]{:S(2)}) async-start(f32[8,160,128]{2,1,0:T(8,128)} %pad_maximum_fusion), calls=%async_computation.3 | async-start | bytes 1310720 | tf_op jit(solution)/shard_map/all_to_all | solution.py:40

commit v2 on v1

--- a/solution.py
+++ b/solution.py
@@ -9,7 +9,14 @@
 
 NZ, NY, NC = 8, 4, 2
 Z_GROUPS = [[z * NY * NC + r for z in range(NZ)] for r in range(NY * NC)]
-Y_GROUPS = [[(z * NY + y) * NC + c for y in range(NY)] for z in range(NZ) for c in range(NC)]
+Y_GROUPS = [[[(z * NY + y) * NC + c for y in range(NY)] for z in range(NZ)] for c in range(NC)]
+QUADS = [
+    [[(z * NY + y) * NC + c for z in range(p, NZ, 2)] for y in range(NY) for p in range(2)]
+    for c in range(NC)
+]
+FIRST = Y_GROUPS[0] + QUADS[1]
+SECOND = QUADS[0] + Y_GROUPS[1]
+YC_GROUPS = [[z * NY * NC + r for r in range(NY * NC)] for z in range(NZ)]
 
 f32 = jnp.float32
 bf16 = jnp.bfloat16
@@ -68,37 +75,62 @@
     width = out_grads.shape[1]
     rows = activations.shape[1]
     panels = rows // block
-    half = panels // NC
-    zr = block // NZ
-    yr = zr // NY
+    quarter = panels // (2 * NC)
+    yr = block // (NZ * NY)
     share = block // n_stat
-    core = position % NC
+    core = jnp.bitwise_and(position, NC - 1)
 
-    partial = lax.dot_general(
-        activations, out_grads, (((0,), (0,)), ((), ())), preferred_element_type=f32
-    ).reshape(NC, half * block, width)
-    give = lax.dynamic_index_in_dim(partial, 1 - core, 0, keepdims=False)
-    keep = lax.dynamic_index_in_dim(partial, core, 0, keepdims=False)
-    got = lax.ppermute(give, "dp", [(i, i ^ 1) for i in range(n_dp)])
-    pair = (keep + got).reshape(half, NZ, zr, width).transpose(1, 0, 2, 3)
-    pair = exchange(pair.astype(bf16).reshape(NZ, half * zr, width), "dp", Z_GROUPS)
-    line = jnp.sum(pair.astype(f32), axis=0).reshape(half, NY, yr, width)
-    line = line.transpose(1, 0, 2, 3).reshape(NY, half * yr, width)
-    owned = jnp.sum(exchange(line, "dp", Y_GROUPS), axis=0)
-    owned = owned.reshape(half, yr * width)
+    def pair_sum(chunk):
+        partial = lax.dot_general(
+            activations[:, chunk * (rows // 2) : (chunk + 1) * (rows // 2)],
+            out_grads,
+            (((0,), (0,)), ((), ())),
+            preferred_element_type=f32,
+        )
+        lower, upper = partial[: rows // 4], partial[rows // 4 :]
+        give = jnp.where(core == 0, upper, lower)
+        got = lax.ppermute(give, "dp", [(i, i ^ 1) for i in range(n_dp)])
+        return jnp.where(core == 0, lower, upper) + got
+
+    def spread(k):
+        x = pair_sum(k).astype(bf16).reshape(quarter, NY, block // NY, width).transpose(1, 0, 2, 3)
+        x = exchange(x.reshape(NY, quarter * block // NY, width), "dp", FIRST)
+        return jnp.sum(x.astype(f32), axis=0).reshape(quarter, NY, 2 * yr, width)
+
+    x = jnp.concatenate([spread(0), spread(1)]).transpose(1, 0, 2, 3)
+    x = exchange(x.reshape(NY, 4 * quarter * yr, width), "dp", SECOND)
+    x = jnp.sum(x, axis=0).reshape(2 * quarter, 2, yr, width)
+    odd = jnp.bitwise_and(position // (NY * NC), 1)
+    even_rows, odd_rows = x[:, 0], x[:, 1]
+    got = lax.ppermute(
+        jnp.where(odd == 0, odd_rows, even_rows),
+        "dp",
+        [(i, i ^ (NY * NC)) for i in range(n_dp)],
+    )
+    owned = (jnp.where(odd == 0, even_rows, odd_rows) + got).reshape(2 * quarter, yr * width)
 
     needs, diag_slot = tables(pattern, holders, position, held, n_dp)
+    kinds = len(needs)
+    needs = jnp.stack(needs, axis=1)
+    mine = jnp.sum(jnp.where(jnp.arange(n_dp)[:, None] == position, needs, 0), axis=0)
     high = owned.astype(bf16)
     low = (owned - high.astype(f32)).astype(bf16)
-    local = jnp.arange(half, dtype=jnp.int32) + core * half
-    sent = []
-    for k, need in enumerate(needs):
-        pick = (need[:, None] == local[None, :]).astype(bf16)
-        sent.append(jnp.dot(pick, low if k == 1 else high, preferred_element_type=f32).astype(bf16))
-    kinds = len(sent)
-    sent = jnp.stack(sent, axis=1).reshape(n_dp, kinds * yr, width)
-    came = exchange(sent, "dp").reshape(NZ * NY, NC, kinds, yr, width)
-    came = (came[:, 0] + came[:, 1]).transpose(1, 0, 2, 3).reshape(kinds, block, width)
+    order = jnp.arange(2 * quarter, dtype=jnp.int32)
+    local = jnp.where(order < quarter, order, order + (panels // 2 - quarter)) + core * quarter
+    local = jnp.concatenate([local, local + panels])
+    wanted = needs + jnp.where(jnp.arange(kinds) == 1, panels, 0)
+    pick = (wanted[:, :, None] == local).astype(bf16).reshape(n_dp * kinds, 4 * quarter)
+    sent = jnp.dot(pick, jnp.concatenate([high, low]), preferred_element_type=f32).astype(bf16)
+    plane = NY * NC
+    sent = exchange(sent.reshape(NZ, plane * kinds * yr, width), "dp", Z_GROUPS)
+    sent = sent.reshape(NZ, plane, kinds * yr, width).transpose(1, 0, 2, 3)
+    sent = exchange(sent.reshape(plane, NZ * kinds * yr, width), "dp", YC_GROUPS)
+    came = sent.reshape(NY, NC, NZ, kinds, yr, width)
+    came = came[:, 0] + came[:, 1]
+    by_y = came.transpose(2, 0, 1, 3, 4).reshape(kinds, block, width)
+    by_z = came.reshape(NY, NZ // 2, 2, kinds, yr, width).transpose(3, 1, 0, 2, 4, 5)
+    by_z = by_z.reshape(kinds, block, width)
+    came = jnp.where((jnp.bitwise_and(mine // quarter, 1) == 0)[:, None, None], by_y, by_z)
 
     def gram_of(a, b):
         return lax.dot_general(a, b, (((1,), (1,)), ((), ())), preferred_element_type=f32)

time: 130 us -> 139 us (1.069)
  the two profiles are of different devices: /device:TPU:1 before, /device:TPU:16 now
where the time goes in v2:
time: 139 us; the launch traced here: 138 us
  waiting for transfers between devices  47.3 us (34%)
  starting transfers between devices  41.4 us (30%)
  blocking collectives  14.9 us (11%)
  matrix products  13.2 us (9%)
  other arithmetic  8.52 us (6%)
  between operations  7.09 us (5%)
  local copies, waits for them, and re-layouts  5.68 us (4%)
    all_to_all x5, waiting for transfers between devices, exchange(): return lax.all_to_all(x, axis, 0, 0, axis_index_groups=groups, tiled=True)  43.9 us
    all_to_all x5, starting transfers between devices, exchange(): return lax.all_to_all(x, axis, 0, 0, axis_index_groups=groups, tiled=True)  34.2 us
    all_to_all x1, blocking collectives, exchange(): return lax.all_to_all(x, axis, 0, 0, axis_index_groups=groups, tiled=True)  14.9 us
    dot_general x2, matrix products, pair_sum(): lax.dot_general(activations[:, chunk * (rows // 2):(chunk + 1) * (rows //...  8.33 us
    ppermute x2, starting transfers between devices, pair_sum(): got = lax.ppermute(give, 'dp', [(i, i ^ 1) for i in range(n_dp)])  4.58 us
    ppermute x1, waiting for transfers between devices, per_device(): lax.ppermute(jnp.where(odd == 0, odd_rows, even_rows), 'dp', [(i, i ^ NY...  3.4 us
  transfers between devices with their start and end apart: 8, of which 6 were waited for; matrix products, arithmetic and copies ran while one was open for 7% of the time, Pallas kernels for 0%

profile of v2, /device:TPU:16, one launch (start us, length us, event | category | flops | bytes accessed | tf_op | source)
XLA Modules:
  0.0 138.2 jit_solution(2734002951776276631)
XLA Ops:
  0.7 0.9 copy-done
  1.6 5.9 %fusion.2 = f32[4096,128]{1,0:T(8,128)S(1)} fusion(bf16[1024,128]{1,0:T(8,128)(2,1)S(1)} %copy-done, bf16[1024,8192]{1,0:T(8,128)(2,1)} %param.5), kind=kOutput, calls=%fused_computation.2 | convolution fusion | flops 1073741824 | bytes 10747904 | tf_op jit(solution)/shard_map/dot_general | solution.py:84
  7.6 2.2 %collective-permute-start = (f32[2048,128]{1,0:T(8,128)S(1)}, f32[2048,128]{1,0:T(8,128)S(1)}, u32[]{:S(2)}, u32[]{:S(2)}) collective-permute-start(f32[2048,128]{1,0:T(8,128)S(1)} %slice_select_fusion.1), channel_id=1, source_target_pairs={{0,8},{8,0},{16,24},{24,16},{32,40},{40,32},{48,56},{56,48},{64,72... | collective-permute-start | bytes 3145736 | tf_op jit(solution)/shard_map/ppermute | solution.py:92
  9.8 2.4 %fusion = f32[4096,128]{1,0:T(8,128)S(1)} fusion(bf16[1024,128]{1,0:T(8,128)(2,1)S(1)} %copy-done, bf16[1024,8192]{1,0:T(8,128)(2,1)S(1)} %copy-done.3), kind=kOutput, calls=%fused_computation | convolution fusion | flops 1073741824 | bytes 10747904 | tf_op jit(solution)/shard_map/dot_general | solution.py:84
  12.3 1.1 slice_select_fusion
  13.4 2.4 %collective-permute-start.1 = (f32[2048,128]{1,0:T(8,128)}, f32[2048,128]{1,0:T(8,128)}, u32[]{:S(2)}, u32[]{:S(2)}) collective-permute-start(f32[2048,128]{1,0:T(8,128)} %slice_select_fusion), channel_id=1, source_target_pairs={{0,8},{8,0},{16,24},{24,16},{32,40},{40,32},{48,56},{56,48},{64,72... | collective-permute-start | bytes 3145736 | tf_op jit(solution)/shard_map/ppermute | solution.py:92
  15.9 0.8 copy.63
  16.8 9.1 %all-to-all-start = ((bf16[4,512,128]{2,1,0:T(8,128)(2,1)}), bf16[4,512,128]{2,1,0:T(8,128)(2,1)S(1)}, u32[]{:S(2)}, u32[]{:S(2)}) async-start(bf16[4,512,128]{2,1,0:T(8,128)(2,1)} %bitcast.13), calls=%async_computation | async-start | bytes 1048576 | tf_op jit(solution)/shard_map/all_to_all | solution.py:47
  26.2 1.5 %add_convert_fusion = bf16[2048,128]{1,0:T(8,128)(2,1)S(1)} fusion(f32[2048,128]{1,0:T(8,128)} %collective-permute-done.1, f32[4096,128]{1,0:T(8,128)S(1)} %fusion, pred[]{:T(512)S(6)} %eq.152), kind=kLoop, calls=%fused_computation.9 | loop fusion | flops 786432 | bytes 3670017 | tf_op jit(solution)/shard_map/convert_element_type | solution.py:96
  28.5 6.4 %all-to-all-done = bf16[4,512,128]{2,1,0:T(8,128)(2,1)S(1)} async-done(((bf16[4,512,128]{2,1,0:T(8,128)(2,1)}), bf16[4,512,128]{2,1,0:T(8,128)(2,1)S(1)}, u32[]{:S(2)}, u32[]{:S(2)}) %all-to-all-start) | async-done | bytes 524320 | tf_op jit(solution)/shard_map/all_to_all | solution.py:47
  34.9 5.9 %all-to-all-start.1 = ((bf16[4,512,128]{2,1,0:T(8,128)(2,1)}), bf16[4,512,128]{2,1,0:T(8,128)(2,1)S(1)}, u32[]{:S(2)}, u32[]{:S(2)}) async-start(bf16[4,512,128]{2,1,0:T(8,128)(2,1)} %bitcast.17), calls=%async_computation.1 | async-start | bytes 1048576 | tf_op jit(solution)/shard_map/all_to_all | solution.py:47
  41.1 8.9 %all-to-all-done.1 = bf16[4,512,128]{2,1,0:T(8,128)(2,1)S(1)} async-done(((bf16[4,512,128]{2,1,0:T(8,128)(2,1)}), bf16[4,512,128]{2,1,0:T(8,128)(2,1)S(1)}, u32[]{:S(2)}, u32[]{:S(2)}) %all-to-all-start.1) | async-done | bytes 524320 | tf_op jit(solution)/shard_map/all_to_all | solution.py:47
  50.9 10.6 %all-to-all-start.2 = ((f32[4,256,128]{2,1,0:T(8,128)}), f32[4,256,128]{2,1,0:T(8,128)S(1)}, u32[]{:S(2)}, u32[]{:S(2)}) async-start(f32[4,256,128]{2,1,0:T(8,128)} %copy_bitcast_fusion), calls=%async_computation.2 | async-start | bytes 1048576 | tf_op jit(solution)/shard_map/all_to_all | solution.py:47
  62.0 11.4 %all-to-all-done.2 = f32[4,256,128]{2,1,0:T(8,128)S(1)} async-done(((f32[4,256,128]{2,1,0:T(8,128)}), f32[4,256,128]{2,1,0:T(8,128)S(1)}, u32[]{:S(2)}, u32[]{:S(2)}) %all-to-all-start.2) | async-done | bytes 524320 | tf_op jit(solution)/shard_map/all_to_all | solution.py:47
  73.5 2.7 %collective-permute-start.2 = (f32[32,4,128]{2,1,0:T(4,128)S(1)}, f32[32,4,128]{2,1,0:T(4,128)S(1)}, u32[]{:S(2)}, u32[]{:S(2)}) collective-permute-start(f32[32,4,128]{2,1,0:T(4,128)S(1)} %select_bitcast_fusion.3), channel_id=1, source_target_pairs={{0,64},{8,72},{16,80},{24,88},{32,96},{40,104},{48,112},{56,120},{... | collective-permute-start | bytes 196616 | tf_op jit(solution)/shard_map/ppermute | solution.py:105
  76.2 3.4 %collective-permute-done.2 = f32[32,4,128]{2,1,0:T(4,128)S(1)} collective-permute-done((f32[32,4,128]{2,1,0:T(4,128)S(1)}, f32[32,4,128]{2,1,0:T(4,128)S(1)}, u32[]{:S(2)}, u32[]{:S(2)}) %collective-permute-start.2) | collective-permute-done | bytes 65568 | tf_op jit(solution)/shard_map/ppermute | solution.py:105
  80.3 14.9 %all_to_all.30 = bf16[8,192,128]{2,1,0:T(8,128)(2,1)S(1)} all-to-all(bf16[8,192,128]{2,1,0:T(8,128)(2,1)S(1)} %reshape.175), channel_id=1, replica_groups={{0,64,128,192,256,320,384,448},{8,72,136,200,264,328,392,456},{16,80,14..., dimensions={0} | all-to-all | bytes 786432 | tf_op jit(solution)/shard_map/all_to_all | solution.py:47
  96.0 4.2 %all-to-all-start.4 = ((bf16[8,192,128]{2,1,0:T(8,128)(2,1)}), bf16[8,192,128]{2,1,0:T(8,128)(2,1)S(1)}, u32[]{:S(2)}, u32[]{:S(2)}) async-start(bf16[8,192,128]{2,1,0:T(8,128)(2,1)} %bitcast.29), calls=%async_computation.4 | async-start | bytes 786432 | tf_op jit(solution)/shard_map/all_to_all | solution.py:47
  100.3 13.0 %all-to-all-done.4 = bf16[8,192,128]{2,1,0:T(8,128)(2,1)S(1)} async-done(((bf16[8,192,128]{2,1,0:T(8,128)(2,1)}), bf16[8,192,128]{2,1,0:T(8,128)(2,1)S(1)}, u32[]{:S(2)}, u32[]{:S(2)}) %all-to-all-start.4) | async-done | bytes 393248 | tf_op jit(solution)/shard_map/all_to_all | solution.py:47
  114.4 0.9 pad_maximum_fusion
  115.3 4.3 %all-to-all-start.5 = ((f32[8,160,128]{2,1,0:T(8,128)}), f32[8,160,128]{2,1,0:T(8,128)S(1)}, u32[]{:S(2)}, u32[]{:S(2)}) async-start(f32[8,160,128]{2,1,0:T(8,128)} %pad_maximum_fusion), calls=%async_computation.5 | async-start | bytes 1310720 | tf_op jit(solution)/shard_map/all_to_all | solution.py:47
  125.4 0.8 constant_dynamic-slice_fusion
  126.4 4.1 %all-to-all-done.5 = f32[8,160,128]{2,1,0:T(8,128)S(1)} async-done(((f32[8,160,128]{2,1,0:T(8,128)}), f32[8,160,128]{2,1,0:T(8,128)S(1)}, u32[]{:S(2)}, u32[]{:S(2)}) %all-to-all-start.5) | async-done | bytes 655392 | tf_op jit(solution)/shard_map/all_to_all | solution.py:47
  136.8 1.4 maximum_add_fusion
  (88 shorter events, 11.6 us)
Async XLA Ops:
  0.6 1.0 copy-start
  1.6 8.3 %copy-start.3 = (bf16[1024,8192]{1,0:T(8,128)(2,1)S(1)}, bf16[1024,8192]{1,0:T(8,128)(2,1)}, u32[]{:S(2)}) copy-start(bf16[1024,8192]{1,0:T(8,128)(2,1)} %param.5) | copy-start | bytes 50331652
  7.6 18.3 %copy-start.2 = (s32[192,2]{0,1:T(2,128)S(1)}, s32[192,2]{0,1:T(2,128)}, u32[]{:S(2)}) copy-start(s32[192,2]{0,1:T(2,128)} %param.8) | copy-start | bytes 4612
  7.6 18.3 %copy-start.1 = (s32[192]{0:T(256)S(1)}, s32[192]{0:T(256)}, u32[]{:S(2)}) copy-start(s32[192]{0:T(256)} %param.9) | copy-start | bytes 2308
  7.6 8.1 %collective-permute-start = (f32[2048,128]{1,0:T(8,128)S(1)}, f32[2048,128]{1,0:T(8,128)S(1)}, u32[]{:S(2)}, u32[]{:S(2)}) collective-permute-start(f32[2048,128]{1,0:T(8,128)S(1)} %slice_select_fusion.1), channel_id=1, source_target_pairs={{0,8},{8,0},{16,24},{24,16},{32,40},{40,32},{48,56},{56,48},{64,72... | collective-permute-start | bytes 3145736 | tf_op jit(solution)/shard_map/ppermute | solution.py:92
  13.4 12.8 %collective-permute-start.1 = (f32[2048,128]{1,0:T(8,128)}, f32[2048,128]{1,0:T(8,128)}, u32[]{:S(2)}, u32[]{:S(2)}) collective-permute-start(f32[2048,128]{1,0:T(8,128)} %slice_select_fusion), channel_id=1, source_target_pairs={{0,8},{8,0},{16,24},{24,16},{32,40},{40,32},{48,56},{56,48},{64,72... | collective-permute-start | bytes 3145736 | tf_op jit(solution)/shard_map/ppermute | solution.py:92
  16.8 18.1 %all-to-all-start = ((bf16[4,512,128]{2,1,0:T(8,128)(2,1)}), bf16[4,512,128]{2,1,0:T(8,128)(2,1)S(1)}, u32[]{:S(2)}, u32[]{:S(2)}) async-start(bf16[4,512,128]{2,1,0:T(8,128)(2,1)} %bitcast.13), calls=%async_computation | async-start | bytes 1048576 | tf_op jit(solution)/shard_map/all_to_all | solution.py:47
  34.9 15.1 %all-to-all-start.1 = ((bf16[4,512,128]{2,1,0:T(8,128)(2,1)}), bf16[4,512,128]{2,1,0:T(8,128)(2,1)S(1)}, u32[]{:S(2)}, u32[]{:S(2)}) async-start(bf16[4,512,128]{2,1,0:T(8,128)(2,1)} %bitcast.17), calls=%async_computation.1 | async-start | bytes 1048576 | tf_op jit(solution)/shard_map/all_to_all | solution.py:47
  50.9 22.5 %all-to-all-start.2 = ((f32[4,256,128]{2,1,0:T(8,128)}), f32[4,256,128]{2,1,0:T(8,128)S(1)}, u32[]{:S(2)}, u32[]{:S(2)}) async-start(f32[4,256,128]{2,1,0:T(8,128)} %copy_bitcast_fusion), calls=%async_computation.2 | async-start | bytes 1048576 | tf_op jit(solution)/shard_map/all_to_all | solution.py:47
  73.5 6.2 %collective-permute-start.2 = (f32[32,4,128]{2,1,0:T(4,128)S(1)}, f32[32,4,128]{2,1,0:T(4,128)S(1)}, u32[]{:S(2)}, u32[]{:S(2)}) collective-permute-start(f32[32,4,128]{2,1,0:T(4,128)S(1)} %select_bitcast_fusion.3), channel_id=1, source_target_pairs={{0,64},{8,72},{16,80},{24,88},{32,96},{40,104},{48,112},{56,120},{... | collective-permute-start | bytes 196616 | tf_op jit(solution)/shard_map/ppermute | solution.py:105
  96.0 17.4 %all-to-all-start.4 = ((bf16[8,192,128]{2,1,0:T(8,128)(2,1)}), bf16[8,192,128]{2,1,0:T(8,128)(2,1)S(1)}, u32[]{:S(2)}, u32[]{:S(2)}) async-start(bf16[8,192,128]{2,1,0:T(8,128)(2,1)} %bitcast.29), calls=%async_computation.4 | async-start | bytes 786432 | tf_op jit(solution)/shard_map/all_to_all | solution.py:47
  115.3 15.3 %all-to-all-start.5 = ((f32[8,160,128]{2,1,0:T(8,128)}), f32[8,160,128]{2,1,0:T(8,128)S(1)}, u32[]{:S(2)}, u32[]{:S(2)}) async-start(f32[8,160,128]{2,1,0:T(8,128)} %pad_maximum_fusion), calls=%async_computation.5 | async-start | bytes 1310720 | tf_op jit(solution)/shard_map/all_to_all | solution.py:47

commit v3 on v1

--- a/solution.py
+++ b/solution.py
@@ -1,15 +1,16 @@
 import jax
 import jax.numpy as jnp
 from jax import lax
+from jax.experimental import pallas as pl
+from jax.experimental.pallas import tpu as pltpu
 from jax.sharding import PartitionSpec as P
 
 ITERS = 5
 beta_stat = 0.6
 damping = 0.75
 
-NZ, NY, NC = 8, 4, 2
-Z_GROUPS = [[z * NY * NC + r for z in range(NZ)] for r in range(NY * NC)]
-Y_GROUPS = [[(z * NY + y) * NC + c for y in range(NY)] for z in range(NZ) for c in range(NC)]
+NC = 2
+INTERPRET = False
 
 f32 = jnp.float32
 bf16 = jnp.bfloat16
@@ -58,47 +59,96 @@
     return needs, diag_slot
 
 
+def regroup(x, low_two, even):
+    v0, v1, v2, v3 = x[0], x[1], x[2], x[3]
+    a0, a2 = jnp.where(low_two, v0, pltpu.roll(v2, 4, 1)), jnp.where(low_two, pltpu.roll(v0, 4, 1), v2)
+    a1, a3 = jnp.where(low_two, v1, pltpu.roll(v3, 4, 1)), jnp.where(low_two, pltpu.roll(v1, 4, 1), v3)
+    b0, b1 = jnp.where(even, a0, pltpu.roll(a1, 2, 1)), jnp.where(even, pltpu.roll(a0, 6, 1), a1)
+    b2, b3 = jnp.where(even, a2, pltpu.roll(a3, 2, 1)), jnp.where(even, pltpu.roll(a2, 6, 1), a3)
+    return b0, b1, b2, b3
+
+
+def combine_kernel(core, keep_a, keep_b, got_a, got_b, out):
+    tiles, width = got_a.shape[1] // 8, got_a.shape[2]
+    sub = lax.broadcasted_iota(jnp.int32, (tiles, 8, width), 1)
+    low_two, even = sub < 4, jnp.bitwise_and(sub, 2) == 0
+    for chunk, (keep, got) in enumerate(((keep_a, got_a), (keep_b, got_b))):
+        groups = [
+            regroup(
+                (keep[g : g + 4] + got[g : g + 4]).reshape(4, tiles, 8, width), low_two, even
+            )
+            for g in (0, 4)
+        ]
+        for j in range(4):
+            both = jnp.concatenate([groups[0][j], groups[1][j]], axis=1).astype(bf16)
+            out[:, j, chunk] = both
+
+
+def combine(core, part_a, part_b, got_a, got_b):
+    panels, rows, width = got_a.shape
+    keep_spec = pl.BlockSpec((8, None, rows, width), lambda i, core: (i, core[0], 0, 0))
+    got_spec = pl.BlockSpec((8, rows, width), lambda i, core: (i, 0, 0))
+    return pl.pallas_call(
+        combine_kernel,
+        out_shape=jax.ShapeDtypeStruct((rows // 8, 4, 2, 2 * panels, width), bf16),
+        grid_spec=pltpu.PrefetchScalarGridSpec(
+            num_scalar_prefetch=1,
+            grid=(panels // 8,),
+            in_specs=[keep_spec, keep_spec, got_spec, got_spec],
+            out_specs=pl.BlockSpec((rows // 8, 4, 2, 16, width), lambda i, core: (0, 0, 0, i, 0)),
+        ),
+        cost_estimate=pl.CostEstimate(
+            flops=2 * panels * rows * width, bytes_accessed=20 * panels * rows * width, transcendentals=0
+        ),
+        compiler_params=pltpu.CompilerParams(vmem_limit_bytes=8 << 20),
+        interpret=INTERPRET,
+    )(core.reshape(1), part_a, part_b, got_a, got_b)
+
+
 def per_device(activations, out_grads, stat_old, pattern, holders):
     position = lax.axis_index("dp")
     stat_pos = lax.axis_index("stat")
     n_stat = lax.axis_size("stat")
-    n_dp = NZ * NY * NC
+    n_dp = lax.axis_size("dp")
+    places = n_dp // NC
     block = stat_old.shape[2]
     held = stat_old.shape[0]
     width = out_grads.shape[1]
     rows = activations.shape[1]
     panels = rows // block
-    half = panels // NC
-    zr = block // NZ
-    yr = zr // NY
+    half = block // NC
     share = block // n_stat
-    core = position % NC
+    core = jnp.bitwise_and(position, NC - 1)
 
-    partial = lax.dot_general(
-        activations, out_grads, (((0,), (0,)), ((), ())), preferred_element_type=f32
-    ).reshape(NC, half * block, width)
-    give = lax.dynamic_index_in_dim(partial, 1 - core, 0, keepdims=False)
-    keep = lax.dynamic_index_in_dim(partial, core, 0, keepdims=False)
-    got = lax.ppermute(give, "dp", [(i, i ^ 1) for i in range(n_dp)])
-    pair = (keep + got).reshape(half, NZ, zr, width).transpose(1, 0, 2, 3)
-    pair = exchange(pair.astype(bf16).reshape(NZ, half * zr, width), "dp", Z_GROUPS)
-    line = jnp.sum(pair.astype(f32), axis=0).reshape(half, NY, yr, width)
-    line = line.transpose(1, 0, 2, 3).reshape(NY, half * yr, width)
-    owned = jnp.sum(exchange(line, "dp", Y_GROUPS), axis=0)
-    owned = owned.reshape(half, yr * width)
+    def product(chunk):
+        partial = lax.dot_general(
+            activations[:, chunk * (rows // 2) : (chunk + 1) * (rows // 2)],
+            out_grads,
+            (((0,), (0,)), ((), ())),
+            preferred_element_type=f32,
+        ).reshape(panels // 2, NC, half, width)
+        give = jnp.where(core == 0, partial[:, 1], partial[:, 0])
+        return partial, lax.ppermute(give, "dp", [(i, i ^ 1) for i in range(n_dp)])
+
+    part_a, got_a = product(0)
+    part_b, got_b = product(1)
+    pair = combine(core, part_a, part_b, got_a, got_b).reshape(places, 2 * panels, width)
+    groups = [[NC * j + c for j in range(places)] for c in range(NC)]
+    owned = jnp.sum(exchange(pair, "dp", groups).astype(f32), axis=0)
 
     needs, diag_slot = tables(pattern, holders, position, held, n_dp)
-    high = owned.astype(bf16)
-    low = (owned - high.astype(f32)).astype(bf16)
-    local = jnp.arange(half, dtype=jnp.int32) + core * half
-    sent = []
-    for k, need in enumerate(needs):
-        pick = (need[:, None] == local[None, :]).astype(bf16)
-        sent.append(jnp.dot(pick, low if k == 1 else high, preferred_element_type=f32).astype(bf16))
-    kinds = len(sent)
-    sent = jnp.stack(sent, axis=1).reshape(n_dp, kinds * yr, width)
-    came = exchange(sent, "dp").reshape(NZ * NY, NC, kinds, yr, width)
-    came = (came[:, 0] + came[:, 1]).transpose(1, 0, 2, 3).reshape(kinds, block, width)
+    kinds = len(needs)
+    padded = 8
+    wanted = 2 * jnp.stack(needs, axis=1)[:, :, None] + jnp.arange(2)
+    wanted = wanted + 2 * panels * (jnp.arange(kinds) == 1).astype(jnp.int32)[:, None]
+    wanted = jnp.pad(wanted, ((0, 0), (0, padded - kinds), (0, 0)), constant_values=-1)
+    pick = wanted.reshape(-1, 1) == jnp.arange(4 * panels, dtype=jnp.int32)
+    high = lax.reduce_precision(owned, 8, 7)
+    source = jnp.concatenate([high, owned - high]).astype(bf16)
+    sent = jnp.dot(pick.astype(bf16), source, preferred_element_type=f32).astype(bf16)
+    came = exchange(sent.reshape(n_dp, 2 * padded, width), "dp")
+    came = came.reshape(places, NC, padded, 2, width).transpose(2, 1, 0, 3, 4)
+    came = came.reshape(padded, block, width)
 
     def gram_of(a, b):
         return lax.dot_general(a, b, (((1,), (1,)), ((), ())), preferred_element_type=f32)

time: 130 us -> 117 us (0.900)
  waiting for transfers between devices: 45 us -> 37.8 us
  local copies, waits for them, and re-layouts: 8.18 us -> 3.05 us
  Pallas kernels: 0 us -> 2.05 us
  other arithmetic: 6.15 us -> 4.75 us
    all_to_all x3 -> x2, waiting for transfers between devices: 41.1 us -> 35.1 us  [exchange(): return lax.all_to_all(x, axis, 0, 0, axis_index_groups=groups, tiled=True)]
    ppermute x1 -> x2, starting transfers between devices: 8.73 us -> 10.9 us  [product(): lax.ppermute(give, 'dp', [(i, i ^ 1) for i in range(n_dp)])]
    pallas_call x0 -> x1, Pallas kernels: none -> 2.05 us  [combine(): pl.pallas_call(combine_kernel, out_shape=jax.ShapeDtypeStruct((rows // 8,...]
    unnamed x9, local copies, waits for them, and re-layouts: 2.95 us -> 1.04 us
    convert_element_type x2 -> x0, other arithmetic: 1.81 us -> none  [the longest x1 1.8 us: per_device(): pair.astype(bf16).reshape(NZ, half * zr, width)]
    squeeze x1 -> x0, local copies, waits for them, and re-layouts: 1.46 us -> none  [per_device(): give = lax.dynamic_index_in_dim(partial, 1 - core, 0, keepdims=False)]
    ppermute x1 -> x2, waiting for transfers between devices: 3.94 us -> 2.62 us  [product(): lax.ppermute(give, 'dp', [(i, i ^ 1) for i in range(n_dp)])]
    all_to_all x3 -> x2, starting transfers between devices: 15.5 us -> 14.4 us  [exchange(): return lax.all_to_all(x, axis, 0, 0, axis_index_groups=groups, tiled=True)]
  transfers between devices with their start and end apart: 4 -> 4, of which waited for: 4 -> 3; matrix products, arithmetic and copies ran while one was open for 2% -> 4% of each run, Pallas kernels for 0% -> 0%
where the time goes in v3:
time: 117 us
  waiting for transfers between devices  37.8 us (32%)
  starting transfers between devices  25.4 us (22%)
  blocking collectives  23.6 us (20%)
  matrix products  13.3 us (11%)
  between operations  7.01 us (6%)
  other arithmetic  4.75 us (4%)
  local copies, waits for them, and re-layouts  3.05 us (3%)
  Pallas kernels  2.05 us (2%)
    all_to_all x2, waiting for transfers between devices, exchange(): return lax.all_to_all(x, axis, 0, 0, axis_index_groups=groups, tiled=True)  35.1 us
    all_to_all x1, blocking collectives, exchange(): return lax.all_to_all(x, axis, 0, 0, axis_index_groups=groups, tiled=True)  23.6 us
    all_to_all x2, starting transfers between devices, exchange(): return lax.all_to_all(x, axis, 0, 0, axis_index_groups=groups, tiled=True)  14.4 us
    ppermute x2, starting transfers between devices, product(): lax.ppermute(give, 'dp', [(i, i ^ 1) for i in range(n_dp)])  10.9 us
    dot_general x2, matrix products, product(): lax.dot_general(activations[:, chunk * (rows // 2):(chunk + 1) * (rows //...  8.38 us
    ppermute x2, waiting for transfers between devices, product(): lax.ppermute(give, 'dp', [(i, i ^ 1) for i in range(n_dp)])  2.62 us
  transfers between devices with their start and end apart: 4, of which 3 were waited for; matrix products, arithmetic and copies ran while one was open for 4% of the time, Pallas kernels for 0%

profile of v3, /device:TPU:1, one launch (start us, length us, event | category | flops | bytes accessed | tf_op | source)
XLA Modules:
  0.0 116.9 jit_solution(12498697793676954175)
XLA Ops:
  0.7 0.9 copy-done
  1.6 5.9 %fusion.2 = f32[4096,128]{1,0:T(8,128)S(1)} fusion(bf16[1024,128]{1,0:T(8,128)(2,1)S(1)} %copy-done, bf16[1024,8192]{1,0:T(8,128)(2,1)} %param.5), kind=kOutput, calls=%fused_computation.2 | convolution fusion | flops 1073741824 | bytes 10747904 | tf_op jit(solution)/shard_map/dot_general | solution.py:124
  7.7 9.0 %collective-permute-start = (f32[32,64,128]{2,1,0:T(8,128)S(1)}, f32[32,64,128]{2,1,0:T(8,128)S(1)}, u32[]{:S(2)}, u32[]{:S(2)}) collective-permute-start(f32[32,64,128]{2,1,0:T(8,128)S(1)} %fusion.8), channel_id=1, source_target_pairs={{0,8},{8,0},{16,24},{24,16},{32,40},{40,32},{48,56},{56,48},{64,72... | collective-permute-start | bytes 3145736 | tf_op jit(solution)/shard_map/ppermute | solution.py:131
  16.8 2.4 %fusion = f32[4096,128]{1,0:T(8,128)S(1)} fusion(bf16[1024,128]{1,0:T(8,128)(2,1)S(1)} %copy-done, bf16[1024,8192]{1,0:T(8,128)(2,1)S(1)} %copy-done.3), kind=kOutput, calls=%fused_computation | convolution fusion | flops 1073741824 | bytes 10747904 | tf_op jit(solution)/shard_map/dot_general | solution.py:124
  19.4 1.9 %collective-permute-start.1 = (f32[32,64,128]{2,1,0:T(8,128)S(1)}, f32[32,64,128]{2,1,0:T(8,128)S(1)}, u32[]{:S(2)}, u32[]{:S(2)}) collective-permute-start(f32[32,64,128]{2,1,0:T(8,128)S(1)} %fusion.6), channel_id=1, source_target_pairs={{0,8},{8,0},{16,24},{24,16},{32,40},{40,32},{48,56},{56,48},{64,72... | collective-permute-start | bytes 3145736 | tf_op jit(solution)/shard_map/ppermute | solution.py:131
  21.3 2.6 %collective-permute-done.1.got_b = f32[32,64,128]{2,1,0:T(8,128)S(1)} collective-permute-done((f32[32,64,128]{2,1,0:T(8,128)S(1)}, f32[32,64,128]{2,1,0:T(8,128)S(1)}, u32[]{:S(2)}, u32[]{:S(2)}) %collective-permute-start.1) | collective-permute-done | bytes 1048608 | tf_op jit(solution)/shard_map/ppermute | solution.py:131
  24.0 2.1 %shard_map.68 = bf16[8,4,2,64,128]{4,3,2,1,0:T(8,128)(2,1)} custom-call(s32[1]{0:T(128)} %bitcast.7.core, f32[32,2,64,128]{3,2,1,0:T(8,128)S(1)} %bitcast.98, f32[32,2,64,128]{3,2,1,0:T(8,128)S(1)} %bitcast.100, f32[32,64,128]{2,1,0:T(8,128)S(1)} %collective-permute-done.got_a, f32[32,64,128]{2,1,0:T(8,128)S(1)} %collective-permute-done.1.got_b), custom_call_target="tpu_custom_call" | custom-call | flops 524288 | bytes 5242880 | tf_op jit(solution)/shard_map/pallas_call | solution.py:91
  26.0 10.3 %all-to-all-start = ((bf16[32,128,128]{2,1,0:T(8,128)(2,1)}), bf16[32,128,128]{2,1,0:T(8,128)(2,1)S(1)}, u32[]{:S(2)}, u32[]{:S(2)}) async-start(bf16[32,128,128]{2,1,0:T(8,128)(2,1)} %bitcast.12), calls=%async_computation | async-start | bytes 2097152 | tf_op jit(solution)/shard_map/all_to_all | solution.py:41
  36.4 0.2 convert_reduce_fusion.1
  37.3 31.4 %all-to-all-done = bf16[32,128,128]{2,1,0:T(8,128)(2,1)S(1)} async-done(((bf16[32,128,128]{2,1,0:T(8,128)(2,1)}), bf16[32,128,128]{2,1,0:T(8,128)(2,1)S(1)}, u32[]{:S(2)}, u32[]{:S(2)}) %all-to-all-start) | async-done | bytes 1048608 | tf_op jit(solution)/shard_map/all_to_all | solution.py:41
  68.8 0.4 convolution_convert_fusion
  69.2 23.6 %all_to_all.15 = bf16[64,16,128]{2,1,0:T(8,128)(2,1)S(1)} all-to-all(bf16[64,16,128]{2,1,0:T(8,128)(2,1)S(1)} %bitcast.105), channel_id=1, replica_groups=mesh['dp'=64,'stat'=8] {'dp'}, dimensions={0} | all-to-all | bytes 524288 | tf_op jit(solution)/shard_map/all_to_all | solution.py:41
  92.8 0.2 copy.54
  93.7 0.9 pad_maximum_fusion
  94.6 4.1 %all-to-all-start.2 = ((f32[8,160,128]{2,1,0:T(8,128)}), f32[8,160,128]{2,1,0:T(8,128)S(1)}, u32[]{:S(2)}, u32[]{:S(2)}) async-start(f32[8,160,128]{2,1,0:T(8,128)} %pad_maximum_fusion), calls=%async_computation.2 | async-start | bytes 1310720 | tf_op jit(solution)/shard_map/all_to_all | solution.py:41
  98.7 0.6 fusion.62
  104.5 0.8 constant_dynamic-slice_fusion
  105.5 3.8 %all-to-all-done.2 = f32[8,160,128]{2,1,0:T(8,128)S(1)} async-done(((f32[8,160,128]{2,1,0:T(8,128)}), f32[8,160,128]{2,1,0:T(8,128)S(1)}, u32[]{:S(2)}, u32[]{:S(2)}) %all-to-all-start.2) | async-done | bytes 655392 | tf_op jit(solution)/shard_map/all_to_all | solution.py:41
  109.6 0.6 multiply_reduce_fusion
  111.8 0.2 fusion.36
  112.3 0.2 fusion.93
  114.0 0.2 fusion.32
  114.7 0.8 fusion.19
  115.5 1.4 %maximum_add_fusion = f32[3,16,128]{2,1,0:T(8,128)} fusion(f32[1,16,128]{2,1,0:T(8,128)S(1)} %copy.47, f32[1,16,128]{2,1,0:T(8,128)S(1)} %copy.46, f32[1,16,128]{2,1,0:T(8,128)S(1)} %copy.45, f32[3,128,128]{2,1,0:T(8,128)} %param.7, s32[]{:T(128)S(6)} %select_n.88), kind=kLoop, calls=%fused_computation.90 | loop fusion | flops 24576 | bytes 73732 | tf_op jit(solution)/shard_map/add | solution.py:179
  (53 shorter events, 5.2 us)
Async XLA Ops:
  0.6 1.0 copy-start
  1.6 15.2 %copy-start.3 = (bf16[1024,8192]{1,0:T(8,128)(2,1)S(1)}, bf16[1024,8192]{1,0:T(8,128)(2,1)}, u32[]{:S(2)}) copy-start(bf16[1024,8192]{1,0:T(8,128)(2,1)} %param.5) | copy-start | bytes 50331652
  7.7 13.6 %collective-permute-start = (f32[32,64,128]{2,1,0:T(8,128)S(1)}, f32[32,64,128]{2,1,0:T(8,128)S(1)}, u32[]{:S(2)}, u32[]{:S(2)}) collective-permute-start(f32[32,64,128]{2,1,0:T(8,128)S(1)} %fusion.8), channel_id=1, source_target_pairs={{0,8},{8,0},{16,24},{24,16},{32,40},{40,32},{48,56},{56,48},{64,72... | collective-permute-start | bytes 3145736 | tf_op jit(solution)/shard_map/ppermute | solution.py:131
  19.2 17.2 %copy-start.2 = (s32[192,2]{0,1:T(2,128)S(1)}, s32[192,2]{0,1:T(2,128)}, u32[]{:S(2)}) copy-start(s32[192,2]{0,1:T(2,128)} %param.8) | copy-start | bytes 4612
  19.2 17.2 %copy-start.1 = (s32[192]{0:T(256)S(1)}, s32[192]{0:T(256)}, u32[]{:S(2)}) copy-start(s32[192]{0:T(256)} %param.9) | copy-start | bytes 2308
  19.4 4.6 %collective-permute-start.1 = (f32[32,64,128]{2,1,0:T(8,128)S(1)}, f32[32,64,128]{2,1,0:T(8,128)S(1)}, u32[]{:S(2)}, u32[]{:S(2)}) collective-permute-start(f32[32,64,128]{2,1,0:T(8,128)S(1)} %fusion.6), channel_id=1, source_target_pairs={{0,8},{8,0},{16,24},{24,16},{32,40},{40,32},{48,56},{56,48},{64,72... | collective-permute-start | bytes 3145736 | tf_op jit(solution)/shard_map/ppermute | solution.py:131
  26.0 42.6 %all-to-all-start = ((bf16[32,128,128]{2,1,0:T(8,128)(2,1)}), bf16[32,128,128]{2,1,0:T(8,128)(2,1)S(1)}, u32[]{:S(2)}, u32[]{:S(2)}) async-start(bf16[32,128,128]{2,1,0:T(8,128)(2,1)} %bitcast.12), calls=%async_computation | async-start | bytes 2097152 | tf_op jit(solution)/shard_map/all_to_all | solution.py:41
  94.6 14.7 %all-to-all-start.2 = ((f32[8,160,128]{2,1,0:T(8,128)}), f32[8,160,128]{2,1,0:T(8,128)S(1)}, u32[]{:S(2)}, u32[]{:S(2)}) async-start(f32[8,160,128]{2,1,0:T(8,128)} %pad_maximum_fusion), calls=%async_computation.2 | async-start | bytes 1310720 | tf_op jit(solution)/shard_map/all_to_all | solution.py:41

commit v4 on v3

--- a/solution.py
+++ b/solution.py
@@ -1,3 +1,5 @@
+import functools
+
 import jax
 import jax.numpy as jnp
 from jax import lax
@@ -9,32 +11,12 @@
 beta_stat = 0.6
 damping = 0.75
 
-NC = 2
+NY, NC = 4, 2
 INTERPRET = False
 
 f32 = jnp.float32
 bf16 = jnp.bfloat16
 HI = lax.Precision.HIGHEST
-
-
-def inverse_root(matrix):
-    size = matrix.shape[0]
-    eye = jnp.eye(size, dtype=matrix.dtype)
-    sym = 0.5 * (matrix + matrix.T) + damping * eye
-    scale = jnp.sqrt(jnp.sum(sym * sym))
-    current = sym / scale
-    result = eye
-    for sweep in range(ITERS):
-        factor = (5.0 * eye - current) * 0.25
-        if sweep == 0:
-            result = factor
-        else:
-            result = jnp.dot(result, factor, precision=HI)
-        if sweep < ITERS - 1:
-            square = jnp.dot(factor, factor, precision=HI)
-            fourth = jnp.dot(square, square, precision=HI)
-            current = jnp.dot(fourth, current, precision=HI)
-    return result * scale ** (-0.25)
 
 
 def exchange(x, axis, groups=None):
@@ -68,14 +50,16 @@
     return b0, b1, b2, b3
 
 
-def combine_kernel(core, keep_a, keep_b, got_a, got_b, out):
+def combine_kernel(keep_a, keep_b, got_a, got_b, out):
     tiles, width = got_a.shape[1] // 8, got_a.shape[2]
     sub = lax.broadcasted_iota(jnp.int32, (tiles, 8, width), 1)
     low_two, even = sub < 4, jnp.bitwise_and(sub, 2) == 0
     for chunk, (keep, got) in enumerate(((keep_a, got_a), (keep_b, got_b))):
         groups = [
             regroup(
-                (keep[g : g + 4] + got[g : g + 4]).reshape(4, tiles, 8, width), low_two, even
+                (keep[g : g + 4] + got[g : g + 4].astype(f32)).reshape(4, tiles, 8, width),
+                low_two,
+                even,
             )
             for g in (0, 4)
         ]
@@ -84,25 +68,111 @@
             out[:, j, chunk] = both
 
 
-def combine(core, part_a, part_b, got_a, got_b):
+def combine(keep_a, keep_b, got_a, got_b):
     panels, rows, width = got_a.shape
-    keep_spec = pl.BlockSpec((8, None, rows, width), lambda i, core: (i, core[0], 0, 0))
-    got_spec = pl.BlockSpec((8, rows, width), lambda i, core: (i, 0, 0))
+    spec = pl.BlockSpec((8, rows, width), lambda i: (i, 0, 0))
     return pl.pallas_call(
         combine_kernel,
         out_shape=jax.ShapeDtypeStruct((rows // 8, 4, 2, 2 * panels, width), bf16),
-        grid_spec=pltpu.PrefetchScalarGridSpec(
-            num_scalar_prefetch=1,
-            grid=(panels // 8,),
-            in_specs=[keep_spec, keep_spec, got_spec, got_spec],
-            out_specs=pl.BlockSpec((rows // 8, 4, 2, 16, width), lambda i, core: (0, 0, 0, i, 0)),
-        ),
+        grid=(panels // 8,),
+        in_specs=[spec] * 4,
+        out_specs=pl.BlockSpec((rows // 8, 4, 2, 16, width), lambda i: (0, 0, 0, i, 0)),
         cost_estimate=pl.CostEstimate(
-            flops=2 * panels * rows * width, bytes_accessed=20 * panels * rows * width, transcendentals=0
+            flops=2 * panels * rows * width, bytes_accessed=16 * panels * rows * width, transcendentals=0
         ),
         compiler_params=pltpu.CompilerParams(vmem_limit_bytes=8 << 20),
         interpret=INTERPRET,
-    )(core.reshape(1), part_a, part_b, got_a, got_b)
+    )(keep_a, keep_b, got_a, got_b)
+
+
+def split_kernel(where, part, got, give, keep):
+    x = (part[...] + got[...]).reshape(got.shape[0], got.shape[1] // 16, 2, 8, got.shape[2])
+    even, odd = x[:, :, 0].reshape(give.shape), x[:, :, 1].reshape(give.shape)
+    mine_even = where[1] == 0
+    give[...] = jnp.where(mine_even, odd, even).astype(bf16)
+    keep[...] = jnp.where(mine_even, even, odd)
+
+
+def split(where, part, got):
+    panels, rows, width = got.shape
+    step = 8
+    out_spec = pl.BlockSpec((step, rows // 2, width), lambda i, where: (i, 0, 0))
+    return pl.pallas_call(
+        split_kernel,
+        out_shape=[
+            jax.ShapeDtypeStruct((panels, rows // 2, width), bf16),
+            jax.ShapeDtypeStruct((panels, rows // 2, width), f32),
+        ],
+        grid_spec=pltpu.PrefetchScalarGridSpec(
+            num_scalar_prefetch=1,
+            grid=(panels // step,),
+            in_specs=[
+                pl.BlockSpec((step, None, rows, width), lambda i, where: (i, where[0], 0, 0)),
+                pl.BlockSpec((step, rows, width), lambda i, where: (i, 0, 0)),
+            ],
+            out_specs=[out_spec, out_spec],
+        ),
+        cost_estimate=pl.CostEstimate(
+            flops=panels * rows * width, bytes_accessed=11 * panels * rows * width, transcendentals=0
+        ),
+        compiler_params=pltpu.CompilerParams(vmem_limit_bytes=8 << 20),
+        interpret=INTERPRET,
+    )(where, part, got)
+
+
+def dot_hi(a, b):
+    return jnp.dot(a, b, precision=HI, preferred_element_type=f32)
+
+
+def finish_kernel(where, grams, old_diag, old_rows, high, low, direction, statistics, *, scale):
+    slot, pos = where[0], where[1]
+    block = old_diag.shape[0]
+    held, share = old_rows.shape[0], old_rows.shape[1]
+    total = grams[0]
+    for i in range(1, grams.shape[0]):
+        total = total + grams[i]
+    total = total * scale
+    row = lax.broadcasted_iota(jnp.int32, (block, block), 0)
+    eye = jnp.where(row == lax.broadcasted_iota(jnp.int32, (block, block), 1), 1.0, 0.0)
+    new = beta_stat * old_diag[...] + total[:block]
+    sym = 0.5 * (new + new.T) + damping * eye
+    norm = jnp.sqrt(jnp.sum(jnp.sum(sym * sym, axis=1, keepdims=True), axis=0, keepdims=True))
+    current = sym / norm
+    result = None
+    for sweep in range(ITERS):
+        factor = (5.0 * eye - current) * 0.25
+        result = factor if sweep == 0 else dot_hi(result, factor)
+        if sweep < ITERS - 1:
+            square = dot_hi(factor, factor)
+            fourth = dot_hi(square, square)
+            current = dot_hi(fourth, current)
+    root = result / jnp.sqrt(jnp.sqrt(norm))
+    direction[...] = dot_hi(root, high[...].astype(f32) + low[...].astype(f32))
+    diag = jnp.zeros((share, block), f32)
+    for p in range(block // share):
+        diag = diag + jnp.where(pos == p, total[p * share : (p + 1) * share], 0.0)
+    for j in range(held):
+        part = diag
+        for m in range(held - 1):
+            at = m + jnp.where(slot <= m, 1, 0)
+            part = jnp.where(at == j, total[block + m * share : block + (m + 1) * share], part)
+        statistics[j] = beta_stat * old_rows[j] + part
+
+
+def finish(where, grams, old_diag, old_rows, high, low, scale):
+    block, width = high.shape
+    vmem = pl.BlockSpec(memory_space=pltpu.VMEM)
+    return pl.pallas_call(
+        functools.partial(finish_kernel, scale=scale),
+        out_shape=[
+            jax.ShapeDtypeStruct((block, width), f32),
+            jax.ShapeDtypeStruct(old_rows.shape, f32),
+        ],
+        in_specs=[pl.BlockSpec(memory_space=pltpu.SMEM)] + [vmem] * 5,
+        out_specs=[vmem, vmem],
+        compiler_params=pltpu.CompilerParams(vmem_limit_bytes=16 << 20),
+        interpret=INTERPRET,
+    )(where, grams, old_diag, old_rows, high, low)
 
 
 def per_device(activations, out_grads, stat_old, pattern, holders):
@@ -132,8 +202,19 @@
 
     part_a, got_a = product(0)
     part_b, got_b = product(1)
-    pair = combine(core, part_a, part_b, got_a, got_b).reshape(places, 2 * panels, width)
-    groups = [[NC * j + c for j in range(places)] for c in range(NC)]
+    neighbour = NY * NC
+    where = jnp.stack([core, jnp.bitwise_and(position // neighbour, 1)])
+    swap = [(i, i ^ neighbour) for i in range(n_dp)]
+    give_a, keep_a = split(where, part_a, got_a)
+    got_a = lax.ppermute(give_a, "dp", swap)
+    give_b, keep_b = split(where, part_b, got_b)
+    got_b = lax.ppermute(give_b, "dp", swap)
+    pair = combine(keep_a, keep_b, got_a, got_b).reshape(places // 2, 2 * panels, width)
+    groups = [
+        [(2 * q + p) * neighbour + y * NC + c for q in range(places // (2 * NY)) for y in range(NY)]
+        for p in range(2)
+        for c in range(NC)
+    ]
     owned = jnp.sum(exchange(pair, "dp", groups).astype(f32), axis=0)
 
     needs, diag_slot = tables(pattern, holders, position, held, n_dp)
@@ -159,24 +240,11 @@
         for m in range(held - 1)
     ]
     grams = exchange(jnp.concatenate([diag] + others, axis=1), "stat")
-    grams = jnp.sum(grams, axis=0) * ((1.0 - beta_stat) / (width * n_stat))
-
     old_diag = lax.dynamic_index_in_dim(stat_old, diag_slot, 0, keepdims=False)
-    new_diag = beta_stat * old_diag + grams[:block]
-    root = inverse_root(new_diag)
-    grad = came[0].astype(f32) + came[1].astype(f32)
-    direction = jnp.dot(root, grad, precision=HI)
-
-    diag_rows = lax.dynamic_slice_in_dim(grams[:block], stat_pos * share, share, 0)
-    slots = []
-    for j in range(held):
-        part = diag_rows
-        for m in range(held - 1):
-            here = (diag_slot != j) & (jnp.where(diag_slot < j, j - 1, j) == m)
-            part = jnp.where(here, grams[block + m * share : block + (m + 1) * share], part)
-        slots.append(part)
     old_rows = lax.dynamic_slice_in_dim(stat_old, stat_pos * share, share, 1)
-    statistics = beta_stat * old_rows + jnp.stack(slots)
+    place = jnp.stack([diag_slot, stat_pos]).astype(jnp.int32)
+    scale = (1.0 - beta_stat) / (width * n_stat)
+    direction, statistics = finish(place, grams, old_diag, old_rows, came[0], came[1], scale)
     return (direction, statistics)
 
 

time: 117 us -> 119 us (1.017)
  Pallas kernels: 2.05 us -> 9.55 us
  waiting for transfers between devices: 37.8 us -> 32.1 us
  starting transfers between devices: 25.4 us -> 30.3 us
  matrix products: 13.3 us -> 9.1 us
  between operations: 7.01 us -> 2.87 us
  local copies, waits for them, and re-layouts: 3.05 us -> 4.83 us
    all_to_all x2, waiting for transfers between devices: 35.1 us -> 23.4 us  [exchange(): return lax.all_to_all(x, axis, 0, 0, axis_index_groups=groups, tiled=True)]
    ppermute x0 -> x2, waiting for transfers between devices: none -> 8.75 us  [the longest x1 5.62 us: per_device(): got_a = lax.ppermute(give_a, 'dp', swap)]
    pallas_call x0 -> x3, Pallas kernels: none -> 8 us  [the longest x1 4.48 us: finish(): pl.pallas_call(functools.partial(finish_kernel, scale=scale), out_shape=[...]
    ppermute x0 -> x2, starting transfers between devices: none -> 5.28 us  [the longest x1 3.36 us: per_device(): got_a = lax.ppermute(give_a, 'dp', swap)]
    dot_general x17 -> x0, matrix products: 4.15 us -> none  [the longest x1 0.84 us: per_device(): direction = jnp.dot(root, grad, precision=HI)]
    ppermute x2, waiting for transfers between devices: 2.62 us -> 0.01 us  [product(): lax.ppermute(give, 'dp', [(i, i ^ 1) for i in range(n_dp)])]
    select_n x2, other arithmetic: 0.35 us -> 2.25 us  [product(): give = jnp.where(core == 0, partial[:, 1], partial[:, 0])]
    unnamed x9 -> x12, local copies, waits for them, and re-layouts: 1.04 us -> 2.55 us
  transfers between devices with their start and end apart: 4 -> 6, of which waited for: 3 -> 4; matrix products, arithmetic and copies ran while one was open for 4% -> 6% of each run, Pallas kernels for 0% -> 3%
where the time goes in v4:
time: 119 us; the launch traced here: 118 us
  waiting for transfers between devices  32.1 us (27%)
  starting transfers between devices  30.3 us (25%)
  blocking collectives  24 us (20%)
  Pallas kernels  9.55 us (8%)
  matrix products  9.1 us (8%)
  other arithmetic  5.18 us (4%)
  local copies, waits for them, and re-layouts  4.83 us (4%)
  between operations  2.87 us (2%)
    all_to_all x1, blocking collectives, exchange(): return lax.all_to_all(x, axis, 0, 0, axis_index_groups=groups, tiled=True)  24 us
    all_to_all x2, waiting for transfers between devices, exchange(): return lax.all_to_all(x, axis, 0, 0, axis_index_groups=groups, tiled=True)  23.4 us
    all_to_all x2, starting transfers between devices, exchange(): return lax.all_to_all(x, axis, 0, 0, axis_index_groups=groups, tiled=True)  14.1 us
    ppermute x2, starting transfers between devices, product(): lax.ppermute(give, 'dp', [(i, i ^ 1) for i in range(n_dp)])  11 us
    dot_general x2, matrix products, product(): lax.dot_general(activations[:, chunk * (rows // 2):(chunk + 1) * (rows //...  8.33 us
    ppermute x1, waiting for transfers between devices, per_device(): got_a = lax.ppermute(give_a, 'dp', swap)  5.62 us
    pallas_call x1, Pallas kernels, finish(): pl.pallas_call(functools.partial(finish_kernel, scale=scale), out_shape=[...  4.48 us
    pallas_call x2, Pallas kernels, split(): pl.pallas_call(split_kernel, out_shape=[jax.ShapeDtypeStruct((panels, row...  3.52 us
  transfers between devices with their start and end apart: 6, of which 4 were waited for; matrix products, arithmetic and copies ran while one was open for 6% of the time, Pallas kernels for 3%

profile of v4, /device:TPU:1, one launch (start us, length us, event | category | flops | bytes accessed | tf_op | source)
XLA Modules:
  0.0 118.0 jit_solution(1710030916669372228)
XLA Ops:
  0.7 0.9 copy-done
  1.6 5.9 %fusion = f32[4096,128]{1,0:T(8,128)S(1)} fusion(bf16[1024,128]{1,0:T(8,128)(2,1)S(1)} %copy-done, bf16[1024,8192]{1,0:T(8,128)(2,1)} %param.5), kind=kOutput, calls=%fused_computation | convolution fusion | flops 1073741824 | bytes 10747904 | tf_op jit(solution)/shard_map/dot_general | solution.py:194
  7.5 1.1 fusion.5
  8.6 9.0 %collective-permute-start.1 = (f32[32,64,128]{2,1,0:T(8,128)}, f32[32,64,128]{2,1,0:T(8,128)}, u32[]{:S(2)}, u32[]{:S(2)}) collective-permute-start(f32[32,64,128]{2,1,0:T(8,128)} %fusion.5), channel_id=1, source_target_pairs={{0,8},{8,0},{16,24},{24,16},{32,40},{40,32},{48,56},{56,48},{64,72... | collective-permute-start | bytes 3145736 | tf_op jit(solution)/shard_map/ppermute | solution.py:201
  17.7 2.4 %fusion.2 = f32[4096,128]{1,0:T(8,128)S(1)} fusion(bf16[1024,128]{1,0:T(8,128)(2,1)S(1)} %copy-done, bf16[1024,8192]{1,0:T(8,128)(2,1)S(1)} %copy-done.5), kind=kOutput, calls=%fused_computation.2 | convolution fusion | flops 1073741824 | bytes 10747904 | tf_op jit(solution)/shard_map/dot_general | solution.py:194
  20.1 1.1 fusion.7
  21.2 2.0 %collective-permute-start = (f32[32,64,128]{2,1,0:T(8,128)}, f32[32,64,128]{2,1,0:T(8,128)S(1)}, u32[]{:S(2)}, u32[]{:S(2)}) collective-permute-start(f32[32,64,128]{2,1,0:T(8,128)} %fusion.7), channel_id=1, source_target_pairs={{0,8},{8,0},{16,24},{24,16},{32,40},{40,32},{48,56},{56,48},{64,72... | collective-permute-start | bytes 3145736 | tf_op jit(solution)/shard_map/ppermute | solution.py:201
  23.3 1.6 %copy-done.2 = f32[4096,128]{1,0:T(8,128)S(1)} copy-done((f32[4096,128]{1,0:T(8,128)S(1)}, f32[4096,128]{1,0:T(8,128)}, u32[]{:S(2)}) %copy-start.2) | copy-done | bytes 2097176
  24.9 2.7 %shard_map.69 = (bf16[32,32,128]{2,1,0:T(8,128)(2,1)S(1)}, f32[32,32,128]{2,1,0:T(8,128)S(1)}) custom-call(s32[2]{0:T(128)S(1)} %pad_add_fusion.1.where, f32[32,2,64,128]{3,2,1,0:T(8,128)S(1)} %bitcast.64, f32[32,64,128]{2,1,0:T(8,128)} %collective-permute-done.1.got), custom_call_target="tpu_custom_call" | custom-call | flops 262144 | bytes 2883584 | tf_op jit(solution)/shard_map/pallas_call | solution.py:100
  27.6 1.9 %collective-permute-start.3 = (bf16[32,32,128]{2,1,0:T(8,128)(2,1)S(1)}, bf16[32,32,128]{2,1,0:T(8,128)(2,1)S(1)}, u32[]{:S(2)}, u32[]{:S(2)}) collective-permute-start(bf16[32,32,128]{2,1,0:T(8,128)(2,1)S(1)} %get-tuple-element.9), channel_id=1, source_target_pairs={{0,64},{8,72},{16,80},{24,88},{32,96},{40,104},{48,112},{56,120},{... | collective-permute-start | bytes 786440 | tf_op jit(solution)/shard_map/ppermute | solution.py:211
  29.5 0.8 shard_map.68
  30.4 3.4 %collective-permute-start.2 = (bf16[32,32,128]{2,1,0:T(8,128)(2,1)S(1)}, bf16[32,32,128]{2,1,0:T(8,128)(2,1)S(1)}, u32[]{:S(2)}, u32[]{:S(2)}) collective-permute-start(bf16[32,32,128]{2,1,0:T(8,128)(2,1)S(1)} %get-tuple-element.8), channel_id=1, source_target_pairs={{0,64},{8,72},{16,80},{24,88},{32,96},{40,104},{48,112},{56,120},{... | collective-permute-start | bytes 786440 | tf_op jit(solution)/shard_map/ppermute | solution.py:209
  33.8 3.1 %collective-permute-done.3.got_b = bf16[32,32,128]{2,1,0:T(8,128)(2,1)S(1)} collective-permute-done((bf16[32,32,128]{2,1,0:T(8,128)(2,1)S(1)}, bf16[32,32,128]{2,1,0:T(8,128)(2,1)S(1)}, u32[]{:S(2)}, u32[]{:S(2)}) %collective-permute-start.3) | collective-permute-done | bytes 262176 | tf_op jit(solution)/shard_map/ppermute | solution.py:211
  36.9 5.6 %collective-permute-done.2.got_a = bf16[32,32,128]{2,1,0:T(8,128)(2,1)S(1)} collective-permute-done((bf16[32,32,128]{2,1,0:T(8,128)(2,1)S(1)}, bf16[32,32,128]{2,1,0:T(8,128)(2,1)S(1)}, u32[]{:S(2)}, u32[]{:S(2)}) %collective-permute-start.2) | collective-permute-done | bytes 262176 | tf_op jit(solution)/shard_map/ppermute | solution.py:209
  42.5 1.6 %shard_map.70 = bf16[4,4,2,64,128]{4,3,2,1,0:T(8,128)(2,1)} custom-call(f32[32,32,128]{2,1,0:T(8,128)S(1)} %get-tuple-element.6.keep_a, f32[32,32,128]{2,1,0:T(8,128)S(1)} %get-tuple-element.7.keep_b, bf16[32,32,128]{2,1,0:T(8,128)(2,1)S(1)} %collective-permute-done.2.got_a, bf16[32,32,128]{2,1,0:T(8,128)(2,1)S(1)} %collective-permute-done.3.got_b), custom_call_target="tpu_custom_call" | custom-call | flops 262144 | bytes 2097152 | tf_op jit(solution)/shard_map/pallas_call | solution.py:74
  44.1 10.0 %all-to-all-start = ((bf16[16,128,128]{2,1,0:T(8,128)(2,1)}), bf16[16,128,128]{2,1,0:T(8,128)(2,1)S(1)}, u32[]{:S(2)}, u32[]{:S(2)}) async-start(bf16[16,128,128]{2,1,0:T(8,128)(2,1)} %bitcast.14), calls=%async_computation | async-start | bytes 1048576 | tf_op jit(solution)/shard_map/all_to_all | solution.py:23
  55.0 17.7 %all-to-all-done = bf16[16,128,128]{2,1,0:T(8,128)(2,1)S(1)} async-done(((bf16[16,128,128]{2,1,0:T(8,128)(2,1)}), bf16[16,128,128]{2,1,0:T(8,128)(2,1)S(1)}, u32[]{:S(2)}, u32[]{:S(2)}) %all-to-all-start) | async-done | bytes 524320 | tf_op jit(solution)/shard_map/all_to_all | solution.py:23
  73.2 24.0 %all_to_all.15 = bf16[64,16,128]{2,1,0:T(8,128)(2,1)S(1)} all-to-all(bf16[64,16,128]{2,1,0:T(8,128)(2,1)S(1)} %bitcast.69), channel_id=1, replica_groups=mesh['dp'=64,'stat'=8] {'dp'}, dimensions={0} | all-to-all | bytes 524288 | tf_op jit(solution)/shard_map/all_to_all | solution.py:23
  98.0 0.9 pad_maximum_fusion
  98.9 4.0 %all-to-all-start.2 = ((f32[8,160,128]{2,1,0:T(8,128)}), f32[8,160,128]{2,1,0:T(8,128)S(1)}, u32[]{:S(2)}, u32[]{:S(2)}) async-start(f32[8,160,128]{2,1,0:T(8,128)} %pad_maximum_fusion), calls=%async_computation.2 | async-start | bytes 1310720 | tf_op jit(solution)/shard_map/all_to_all | solution.py:23
  106.2 0.7 constant_dynamic-slice_fusion.old_rows
  107.0 0.8 dynamic-slice_bitcast_fusion.old_diag
  107.8 5.7 %all-to-all-done.2.grams = f32[8,160,128]{2,1,0:T(8,128)S(1)} async-done(((f32[8,160,128]{2,1,0:T(8,128)}), f32[8,160,128]{2,1,0:T(8,128)S(1)}, u32[]{:S(2)}, u32[]{:S(2)}) %all-to-all-start.2) | async-done | bytes 655392 | tf_op jit(solution)/shard_map/all_to_all | solution.py:23
  113.5 4.5 %shard_map.71 = (f32[128,128]{1,0:T(8,128)}, f32[3,16,128]{2,1,0:T(8,128)}) custom-call(s32[2]{0:T(128)S(1)} %pad_add_fusion.where, f32[8,160,128]{2,1,0:T(8,128)S(1)} %all-to-all-done.2.grams, f32[128,128]{1,0:T(8,128)S(1)} %dynamic-slice_bitcast_fusion.old_diag, f32[3,16,128]{2,1,0:T(8,128)S(1)} %constant_dynamic-slice_fusion.old_rows, ...), custom_call_target="tpu_custom_call" | custom-call | tf_op jit(solution)/shard_map/pallas_call | solution.py:165
  (42 shorter events, 3.6 us)
Async XLA Ops:
  0.6 1.0 copy-start
  1.6 16.1 %copy-start.5 = (bf16[1024,8192]{1,0:T(8,128)(2,1)S(1)}, bf16[1024,8192]{1,0:T(8,128)(2,1)}, u32[]{:S(2)}) copy-start(bf16[1024,8192]{1,0:T(8,128)(2,1)} %param.5) | copy-start | bytes 50331652
  7.5 12.6 %copy-start.1 = (f32[4096,128]{1,0:T(8,128)}, f32[4096,128]{1,0:T(8,128)S(1)}, u32[]{:S(2)}) copy-start(f32[4096,128]{1,0:T(8,128)S(1)} %fusion) | copy-start | bytes 6291460
  8.6 14.7 %collective-permute-start.1 = (f32[32,64,128]{2,1,0:T(8,128)}, f32[32,64,128]{2,1,0:T(8,128)}, u32[]{:S(2)}, u32[]{:S(2)}) collective-permute-start(f32[32,64,128]{2,1,0:T(8,128)} %fusion.5), channel_id=1, source_target_pairs={{0,8},{8,0},{16,24},{24,16},{32,40},{40,32},{48,56},{56,48},{64,72... | collective-permute-start | bytes 3145736 | tf_op jit(solution)/shard_map/ppermute | solution.py:201
  20.1 13.7 %copy-start.4 = (s32[192,2]{0,1:T(2,128)S(1)}, s32[192,2]{0,1:T(2,128)}, u32[]{:S(2)}) copy-start(s32[192,2]{0,1:T(2,128)} %param.8) | copy-start | bytes 4612
  20.1 34.0 %copy-start.3 = (s32[192]{0:T(256)S(1)}, s32[192]{0:T(256)}, u32[]{:S(2)}) copy-start(s32[192]{0:T(256)} %param.9) | copy-start | bytes 2308
  21.2 8.3 %collective-permute-start = (f32[32,64,128]{2,1,0:T(8,128)}, f32[32,64,128]{2,1,0:T(8,128)S(1)}, u32[]{:S(2)}, u32[]{:S(2)}) collective-permute-start(f32[32,64,128]{2,1,0:T(8,128)} %fusion.7), channel_id=1, source_target_pairs={{0,8},{8,0},{16,24},{24,16},{32,40},{40,32},{48,56},{56,48},{64,72... | collective-permute-start | bytes 3145736 | tf_op jit(solution)/shard_map/ppermute | solution.py:201
  23.3 1.6 %copy-start.2 = (f32[4096,128]{1,0:T(8,128)S(1)}, f32[4096,128]{1,0:T(8,128)}, u32[]{:S(2)}) copy-start(f32[4096,128]{1,0:T(8,128)} %copy-done.1) | copy-start | bytes 6291460
  27.6 9.3 %collective-permute-start.3 = (bf16[32,32,128]{2,1,0:T(8,128)(2,1)S(1)}, bf16[32,32,128]{2,1,0:T(8,128)(2,1)S(1)}, u32[]{:S(2)}, u32[]{:S(2)}) collective-permute-start(bf16[32,32,128]{2,1,0:T(8,128)(2,1)S(1)} %get-tuple-element.9), channel_id=1, source_target_pairs={{0,64},{8,72},{16,80},{24,88},{32,96},{40,104},{48,112},{56,120},{... | collective-permute-start | bytes 786440 | tf_op jit(solution)/shard_map/ppermute | solution.py:211
  30.4 12.2 %collective-permute-start.2 = (bf16[32,32,128]{2,1,0:T(8,128)(2,1)S(1)}, bf16[32,32,128]{2,1,0:T(8,128)(2,1)S(1)}, u32[]{:S(2)}, u32[]{:S(2)}) collective-permute-start(bf16[32,32,128]{2,1,0:T(8,128)(2,1)S(1)} %get-tuple-element.8), channel_id=1, source_target_pairs={{0,64},{8,72},{16,80},{24,88},{32,96},{40,104},{48,112},{56,120},{... | collective-permute-start | bytes 786440 | tf_op jit(solution)/shard_map/ppermute | solution.py:209
  44.1 28.7 %all-to-all-start = ((bf16[16,128,128]{2,1,0:T(8,128)(2,1)}), bf16[16,128,128]{2,1,0:T(8,128)(2,1)S(1)}, u32[]{:S(2)}, u32[]{:S(2)}) async-start(bf16[16,128,128]{2,1,0:T(8,128)(2,1)} %bitcast.14), calls=%async_computation | async-start | bytes 1048576 | tf_op jit(solution)/shard_map/all_to_all | solution.py:23
  98.9 14.6 %all-to-all-start.2 = ((f32[8,160,128]{2,1,0:T(8,128)}), f32[8,160,128]{2,1,0:T(8,128)S(1)}, u32[]{:S(2)}, u32[]{:S(2)}) async-start(f32[8,160,128]{2,1,0:T(8,128)} %pad_maximum_fusion), calls=%async_computation.2 | async-start | bytes 1310720 | tf_op jit(solution)/shard_map/all_to_all | solution.py:23

commit v5 on v3

--- a/solution.py
+++ b/solution.py
@@ -1,3 +1,5 @@
+import functools
+
 import jax
 import jax.numpy as jnp
 from jax import lax
@@ -15,26 +17,6 @@
 f32 = jnp.float32
 bf16 = jnp.bfloat16
 HI = lax.Precision.HIGHEST
-
-
-def inverse_root(matrix):
-    size = matrix.shape[0]
-    eye = jnp.eye(size, dtype=matrix.dtype)
-    sym = 0.5 * (matrix + matrix.T) + damping * eye
-    scale = jnp.sqrt(jnp.sum(sym * sym))
-    current = sym / scale
-    result = eye
-    for sweep in range(ITERS):
-        factor = (5.0 * eye - current) * 0.25
-        if sweep == 0:
-            result = factor
-        else:
-            result = jnp.dot(result, factor, precision=HI)
-        if sweep < ITERS - 1:
-            square = jnp.dot(factor, factor, precision=HI)
-            fourth = jnp.dot(square, square, precision=HI)
-            current = jnp.dot(fourth, current, precision=HI)
-    return result * scale ** (-0.25)
 
 
 def exchange(x, axis, groups=None):
@@ -105,6 +87,66 @@
     )(core.reshape(1), part_a, part_b, got_a, got_b)
 
 
+def dot_hi(a, b):
+    return jnp.dot(a, b, precision=HI, preferred_element_type=f32)
+
+
+def finish_kernel(where, came, old_diag, old_rows, high, low, direction, statistics, *, scale):
+    slot, pos = where[0], where[1]
+    block = old_diag.shape[0]
+    held, share = old_rows.shape[0], old_rows.shape[1]
+    diag_gram = jnp.zeros((block, block), f32)
+    rest = jnp.zeros((came.shape[1] - block, block), f32)
+    for i in range(came.shape[0]):
+        panel = came[i, :block]
+        diag_gram = diag_gram + lax.dot_general(
+            panel, panel, (((1,), (1,)), ((), ())), preferred_element_type=f32
+        )
+        rest = rest + came[i, block:].astype(f32)
+    diag_gram, rest = diag_gram * scale, rest * scale
+    row = lax.broadcasted_iota(jnp.int32, (block, block), 0)
+    eye = jnp.where(row == lax.broadcasted_iota(jnp.int32, (block, block), 1), 1.0, 0.0)
+    new = beta_stat * old_diag[...] + diag_gram
+    sym = 0.5 * (new + new.T) + damping * eye
+    norm = jnp.sqrt(jnp.sum(jnp.sum(sym * sym, axis=1, keepdims=True), axis=0, keepdims=True))
+    current = sym / norm
+    result = None
+    for sweep in range(ITERS):
+        factor = (5.0 * eye - current) * 0.25
+        result = factor if sweep == 0 else dot_hi(result, factor)
+        if sweep < ITERS - 1:
+            square = dot_hi(factor, factor)
+            fourth = dot_hi(square, square)
+            current = dot_hi(fourth, current)
+    root = result / jnp.sqrt(jnp.sqrt(norm))
+    direction[...] = dot_hi(root, high[...].astype(f32) + low[...].astype(f32))
+    diag = jnp.zeros((share, block), f32)
+    for p in range(block // share):
+        diag = diag + jnp.where(pos == p, diag_gram[p * share : (p + 1) * share], 0.0)
+    for j in range(held):
+        part = diag
+        for m in range(held - 1):
+            at = m + jnp.where(slot <= m, 1, 0)
+            part = jnp.where(at == j, rest[m * share : (m + 1) * share], part)
+        statistics[j] = beta_stat * old_rows[j] + part
+
+
+def finish(where, came, old_diag, old_rows, high, low, scale):
+    block, width = high.shape
+    vmem = pl.BlockSpec(memory_space=pltpu.VMEM)
+    return pl.pallas_call(
+        functools.partial(finish_kernel, scale=scale),
+        out_shape=[
+            jax.ShapeDtypeStruct((block, width), f32),
+            jax.ShapeDtypeStruct(old_rows.shape, f32),
+        ],
+        in_specs=[pl.BlockSpec(memory_space=pltpu.SMEM)] + [vmem] * 5,
+        out_specs=[vmem, vmem],
+        compiler_params=pltpu.CompilerParams(vmem_limit_bytes=16 << 20),
+        interpret=INTERPRET,
+    )(where, came, old_diag, old_rows, high, low)
+
+
 def per_device(activations, out_grads, stat_old, pattern, holders):
     position = lax.axis_index("dp")
     stat_pos = lax.axis_index("stat")
@@ -137,6 +179,10 @@
     owned = jnp.sum(exchange(pair, "dp", groups).astype(f32), axis=0)
 
     needs, diag_slot = tables(pattern, holders, position, held, n_dp)
+    old_diag = lax.dynamic_index_in_dim(stat_old, diag_slot, 0, keepdims=False)
+    old_rows = lax.dynamic_slice_in_dim(stat_old, stat_pos * share, share, 1)
+    place = jnp.stack([diag_slot, stat_pos]).astype(jnp.int32)
+    owned, old_diag, old_rows, place = lax.optimization_barrier((owned, old_diag, old_rows, place))
     kinds = len(needs)
     padded = 8
     wanted = 2 * jnp.stack(needs, axis=1)[:, :, None] + jnp.arange(2)
@@ -153,30 +199,14 @@
     def gram_of(a, b):
         return lax.dot_general(a, b, (((1,), (1,)), ((), ())), preferred_element_type=f32)
 
-    diag = jnp.broadcast_to(gram_of(came[0], came[0])[None], (n_stat, block, block))
+    own = jnp.broadcast_to(came[0][None], (n_stat, block, width))
     others = [
-        gram_of(came[2 + 2 * m], came[3 + 2 * m]).reshape(n_stat, share, block)
+        gram_of(came[2 + 2 * m], came[3 + 2 * m]).astype(bf16).reshape(n_stat, share, block)
         for m in range(held - 1)
     ]
-    grams = exchange(jnp.concatenate([diag] + others, axis=1), "stat")
-    grams = jnp.sum(grams, axis=0) * ((1.0 - beta_stat) / (width * n_stat))
-
-    old_diag = lax.dynamic_index_in_dim(stat_old, diag_slot, 0, keepdims=False)
-    new_diag = beta_stat * old_diag + grams[:block]
-    root = inverse_root(new_diag)
-    grad = came[0].astype(f32) + came[1].astype(f32)
-    direction = jnp.dot(root, grad, precision=HI)
-
-    diag_rows = lax.dynamic_slice_in_dim(grams[:block], stat_pos * share, share, 0)
-    slots = []
-    for j in range(held):
-        part = diag_rows
-        for m in range(held - 1):
-            here = (diag_slot != j) & (jnp.where(diag_slot < j, j - 1, j) == m)
-            part = jnp.where(here, grams[block + m * share : block + (m + 1) * share], part)
-        slots.append(part)
-    old_rows = lax.dynamic_slice_in_dim(stat_old, stat_pos * share, share, 1)
-    statistics = beta_stat * old_rows + jnp.stack(slots)
+    gathered = exchange(jnp.concatenate([own] + others, axis=1), "stat")
+    scale = (1.0 - beta_stat) / (width * n_stat)
+    direction, statistics = finish(place, gathered, old_diag, old_rows, came[0], came[1], scale)
     return (direction, statistics)
 
 

time: 117 us -> 114 us (0.974)
  Pallas kernels: 2.05 us -> 6.87 us
  between operations: 7.01 us -> 2.82 us
  other arithmetic: 4.75 us -> 3.12 us
  waiting for transfers between devices: 37.8 us -> 36.4 us
    pallas_call x0 -> x1, Pallas kernels: none -> 4.88 us  [finish(): pl.pallas_call(functools.partial(finish_kernel, scale=scale), out_shape=[...]
    dot_general x17 -> x0, matrix products: 4.15 us -> none  [the longest x1 0.84 us: per_device(): direction = jnp.dot(root, grad, precision=HI)]
    dot_general x2, matrix products: 8.38 us -> 11.6 us  [product(): lax.dot_general(activations[:, chunk * (rows // 2):(chunk + 1) * (rows //...]
    all_to_all x2, waiting for transfers between devices: 35.1 us -> 33.8 us  [exchange(): return lax.all_to_all(x, axis, 0, 0, axis_index_groups=groups, tiled=True)]
    add x1 -> x0, other arithmetic: 1.35 us -> none  [per_device(): statistics = beta_stat * old_rows + jnp.stack(slots)]
  transfers between devices with their start and end apart: 4 -> 4, of which waited for: 3 -> 3; matrix products, arithmetic and copies ran while one was open for 4% -> 9% of each run, Pallas kernels for 0% -> 0%
where the time goes in v5:
time: 114 us; the launch traced here: 113 us
  waiting for transfers between devices  36.4 us (32%)
  starting transfers between devices  25 us (22%)
  blocking collectives  23.7 us (21%)
  matrix products  12.2 us (11%)
  Pallas kernels  6.87 us (6%)
  local copies, waits for them, and re-layouts  3.21 us (3%)
  other arithmetic  3.12 us (3%)
  between operations  2.82 us (2%)
    all_to_all x2, waiting for transfers between devices, exchange(): return lax.all_to_all(x, axis, 0, 0, axis_index_groups=groups, tiled=True)  33.8 us
    all_to_all x1, blocking collectives, exchange(): return lax.all_to_all(x, axis, 0, 0, axis_index_groups=groups, tiled=True)  23.7 us
    all_to_all x2, starting transfers between devices, exchange(): return lax.all_to_all(x, axis, 0, 0, axis_index_groups=groups, tiled=True)  14.3 us
    dot_general x2, matrix products, product(): lax.dot_general(activations[:, chunk * (rows // 2):(chunk + 1) * (rows //...  11.6 us
    ppermute x2, starting transfers between devices, product(): lax.ppermute(give, 'dp', [(i, i ^ 1) for i in range(n_dp)])  10.7 us
    pallas_call x1, Pallas kernels, finish(): pl.pallas_call(functools.partial(finish_kernel, scale=scale), out_shape=[...  4.88 us
    ppermute x2, waiting for transfers between devices, product(): lax.ppermute(give, 'dp', [(i, i ^ 1) for i in range(n_dp)])  2.62 us
  transfers between devices with their start and end apart: 4, of which 3 were waited for; matrix products, arithmetic and copies ran while one was open for 9% of the time, Pallas kernels for 0%

profile of v5, /device:TPU:1, one launch (start us, length us, event | category | flops | bytes accessed | tf_op | source)
XLA Modules:
  0.0 113.3 jit_solution(7574690372892159884)
XLA Ops:
  0.7 0.9 copy-done
  1.6 5.8 %fusion.2 = f32[4096,128]{1,0:T(8,128)S(1)} fusion(bf16[1024,128]{1,0:T(8,128)(2,1)S(1)} %copy-done, bf16[1024,8192]{1,0:T(8,128)(2,1)} %param.5), kind=kOutput, calls=%fused_computation.2 | convolution fusion | flops 1073741824 | bytes 10747904 | tf_op jit(solution)/shard_map/dot_general | solution.py:166
  7.5 8.7 %collective-permute-start = (f32[32,64,128]{2,1,0:T(8,128)S(1)}, f32[32,64,128]{2,1,0:T(8,128)S(1)}, u32[]{:S(2)}, u32[]{:S(2)}) collective-permute-start(f32[32,64,128]{2,1,0:T(8,128)S(1)} %fusion.7), channel_id=1, source_target_pairs={{0,8},{8,0},{16,24},{24,16},{32,40},{40,32},{48,56},{56,48},{64,72... | collective-permute-start | bytes 3145736 | tf_op jit(solution)/shard_map/ppermute | solution.py:173
  16.3 5.8 %fusion = f32[4096,128]{1,0:T(8,128)S(1)} fusion(bf16[1024,128]{1,0:T(8,128)(2,1)S(1)} %copy-done, bf16[1024,8192]{1,0:T(8,128)(2,1)} %param.5), kind=kOutput, calls=%fused_computation | convolution fusion | flops 1073741824 | bytes 10747904 | tf_op jit(solution)/shard_map/dot_general | solution.py:166
  22.1 0.2 fusion.5
  22.3 1.9 %collective-permute-start.1 = (f32[32,64,128]{2,1,0:T(8,128)S(1)}, f32[32,64,128]{2,1,0:T(8,128)S(1)}, u32[]{:S(2)}, u32[]{:S(2)}) collective-permute-start(f32[32,64,128]{2,1,0:T(8,128)S(1)} %fusion.5), channel_id=1, source_target_pairs={{0,8},{8,0},{16,24},{24,16},{32,40},{40,32},{48,56},{56,48},{64,72... | collective-permute-start | bytes 3145736 | tf_op jit(solution)/shard_map/ppermute | solution.py:173
  24.3 2.6 %collective-permute-done.1.got_b = f32[32,64,128]{2,1,0:T(8,128)S(1)} collective-permute-done((f32[32,64,128]{2,1,0:T(8,128)S(1)}, f32[32,64,128]{2,1,0:T(8,128)S(1)}, u32[]{:S(2)}, u32[]{:S(2)}) %collective-permute-start.1) | collective-permute-done | bytes 1048608 | tf_op jit(solution)/shard_map/ppermute | solution.py:173
  26.9 2.0 %shard_map.68 = bf16[8,4,2,64,128]{4,3,2,1,0:T(8,128)(2,1)} custom-call(s32[1]{0:T(128)} %bitcast.core, f32[32,2,64,128]{3,2,1,0:T(8,128)S(1)} %bitcast.57, f32[32,2,64,128]{3,2,1,0:T(8,128)S(1)} %bitcast.59, f32[32,64,128]{2,1,0:T(8,128)S(1)} %collective-permute-done.got_a, f32[32,64,128]{2,1,0:T(8,128)S(1)} %collective-permute-done.1.got_b), custom_call_target="tpu_custom_call" | custom-call | flops 524288 | bytes 5242880 | tf_op jit(solution)/shard_map/pallas_call | solution.py:73
  28.9 10.3 %all-to-all-start = ((bf16[32,128,128]{2,1,0:T(8,128)(2,1)}), bf16[32,128,128]{2,1,0:T(8,128)(2,1)S(1)}, u32[]{:S(2)}, u32[]{:S(2)}) async-start(bf16[32,128,128]{2,1,0:T(8,128)(2,1)} %bitcast.5), calls=%async_computation | async-start | bytes 2097152 | tf_op jit(solution)/shard_map/all_to_all | solution.py:23
  39.3 0.2 convert_reduce_fusion.1
  39.5 0.6 fusion.17
  41.4 0.2 select_reduce_fusion.1
  41.9 0.2 eq.92
  42.7 0.7 pad_add_fusion.where
  43.5 0.7 constant_dynamic-slice_fusion.old_rows
  44.2 0.8 dynamic-slice_bitcast_fusion.old_diag
  45.0 26.4 %all-to-all-done = bf16[32,128,128]{2,1,0:T(8,128)(2,1)S(1)} async-done(((bf16[32,128,128]{2,1,0:T(8,128)(2,1)}), bf16[32,128,128]{2,1,0:T(8,128)(2,1)S(1)}, u32[]{:S(2)}, u32[]{:S(2)}) %all-to-all-start) | async-done | bytes 1048608 | tf_op jit(solution)/shard_map/all_to_all | solution.py:23
  71.4 0.2 convert_reduce_fusion
  71.6 0.4 convolution_convert_fusion
  72.0 23.7 %all_to_all.15 = bf16[64,16,128]{2,1,0:T(8,128)(2,1)S(1)} all-to-all(bf16[64,16,128]{2,1,0:T(8,128)(2,1)S(1)} %bitcast.64), channel_id=1, replica_groups=mesh['dp'=64,'stat'=8] {'dp'}, dimensions={0} | all-to-all | bytes 524288 | tf_op jit(solution)/shard_map/all_to_all | solution.py:23
  96.4 0.7 pad_maximum_fusion
  97.1 4.0 %all-to-all-start.2 = ((bf16[8,160,128]{2,1,0:T(8,128)(2,1)}), bf16[8,160,128]{2,1,0:T(8,128)(2,1)S(1)}, u32[]{:S(2)}, u32[]{:S(2)}) async-start(bf16[8,160,128]{2,1,0:T(8,128)(2,1)} %pad_maximum_fusion), calls=%async_computation.2 | async-start | bytes 655360 | tf_op jit(solution)/shard_map/all_to_all | solution.py:23
  101.1 7.4 %all-to-all-done.2.came = bf16[8,160,128]{2,1,0:T(8,128)(2,1)S(1)} async-done(((bf16[8,160,128]{2,1,0:T(8,128)(2,1)}), bf16[8,160,128]{2,1,0:T(8,128)(2,1)S(1)}, u32[]{:S(2)}, u32[]{:S(2)}) %all-to-all-start.2) | async-done | bytes 327712 | tf_op jit(solution)/shard_map/all_to_all | solution.py:23
  108.5 4.9 %shard_map.69 = (f32[128,128]{1,0:T(8,128)}, f32[3,16,128]{2,1,0:T(8,128)}) custom-call(s32[2]{0:T(128)S(1)} %pad_add_fusion.where, bf16[8,160,128]{2,1,0:T(8,128)(2,1)S(1)} %all-to-all-done.2.came, f32[128,128]{1,0:T(8,128)S(1)} %dynamic-slice_bitcast_fusion.old_diag, f32[3,16,128]{2,1,0:T(8,128)S(1)} %constant_dynamic-slice_fusion.old_rows, ...), custom_call_target="tpu_custom_call" | custom-call | tf_op jit(solution)/shard_map/pallas_call | solution.py:137
  (28 shorter events, 1.1 us)
Async XLA Ops:
  0.6 1.0 copy-start
  7.5 16.7 %collective-permute-start = (f32[32,64,128]{2,1,0:T(8,128)S(1)}, f32[32,64,128]{2,1,0:T(8,128)S(1)}, u32[]{:S(2)}, u32[]{:S(2)}) collective-permute-start(f32[32,64,128]{2,1,0:T(8,128)S(1)} %fusion.7), channel_id=1, source_target_pairs={{0,8},{8,0},{16,24},{24,16},{32,40},{40,32},{48,56},{56,48},{64,72... | collective-permute-start | bytes 3145736 | tf_op jit(solution)/shard_map/ppermute | solution.py:173
  22.1 17.1 %copy-start.2 = (s32[192,2]{0,1:T(2,128)S(1)}, s32[192,2]{0,1:T(2,128)}, u32[]{:S(2)}) copy-start(s32[192,2]{0,1:T(2,128)} %param.8) | copy-start | bytes 4612
  22.1 17.1 %copy-start.1 = (s32[192]{0:T(256)S(1)}, s32[192]{0:T(256)}, u32[]{:S(2)}) copy-start(s32[192]{0:T(256)} %param.9) | copy-start | bytes 2308
  22.3 4.6 %collective-permute-start.1 = (f32[32,64,128]{2,1,0:T(8,128)S(1)}, f32[32,64,128]{2,1,0:T(8,128)S(1)}, u32[]{:S(2)}, u32[]{:S(2)}) collective-permute-start(f32[32,64,128]{2,1,0:T(8,128)S(1)} %fusion.5), channel_id=1, source_target_pairs={{0,8},{8,0},{16,24},{24,16},{32,40},{40,32},{48,56},{56,48},{64,72... | collective-permute-start | bytes 3145736 | tf_op jit(solution)/shard_map/ppermute | solution.py:173
  28.9 42.6 %all-to-all-start = ((bf16[32,128,128]{2,1,0:T(8,128)(2,1)}), bf16[32,128,128]{2,1,0:T(8,128)(2,1)S(1)}, u32[]{:S(2)}, u32[]{:S(2)}) async-start(bf16[32,128,128]{2,1,0:T(8,128)(2,1)} %bitcast.5), calls=%async_computation | async-start | bytes 2097152 | tf_op jit(solution)/shard_map/all_to_all | solution.py:23
  97.1 11.4 %all-to-all-start.2 = ((bf16[8,160,128]{2,1,0:T(8,128)(2,1)}), bf16[8,160,128]{2,1,0:T(8,128)(2,1)S(1)}, u32[]{:S(2)}, u32[]{:S(2)}) async-start(bf16[8,160,128]{2,1,0:T(8,128)(2,1)} %pad_maximum_fusion), calls=%async_computation.2 | async-start | bytes 655360 | tf_op jit(solution)/shard_map/all_to_all | solution.py:23
